TPU v7x, 32 devices: a whole 2x2x4 slice. The times are simulated.
32 devices in a mesh: parts: 2 (over x), gx: 4 (over y, core), gy: 4 (over z).
Axes of the slice: x: 2, y: 2, z: 4, core: 2. Of those that a mesh axis runs over, the one named last changes fastest.
Arguments:
- forcing_right_side: float32 [32, 32, 1024], P(('parts', 'gx'), 'gy'), parts along dimension 0, may hold values from -18 to 18
- earlier_warmth: float32 [32, 32, 1024], P(('parts', 'gx'), 'gy'), parts along dimension 0, may hold values from 0 to 2
- matter_condition: int32 [32, 32, 1024], P(('parts', 'gx'), 'gy'), parts along dimension 0, may hold values from 0 to 2
- compressed_slot_number: int32 [32, 32, 1024], P(('parts', 'gx'), 'gy'), parts along dimension 0, may hold values from 0 to 127
- normal_draw_factor: float32 [32, 32, 1024], P(('parts', 'gx'), 'gy'), parts along dimension 0, may hold values from -6 to 6
Outputs:
- solution: float32 [32, 32, 1024], P(('parts', 'gx'), 'gy'), parts along dimension 0
- residual: float32 [32, 32, 1024], P(('parts', 'gx'), 'gy'), parts along dimension 0
There are 2 independent parts, one for each index of `parts`. A program takes and returns all parts, laid end to end along the dimension named above; each array names one. Nothing has to cross between parts.
Inputs may be any that keep to these rules, and one draw needn't show every extreme that they name: `matter_condition`: phase labels the cell as powder, solid or liquid. `compressed_slot_number`: each cell's row of the sketch.
All inputs are finite; a program needn't handle non-finite values.
Results may differ from a plain program's by a relative error of at most 0.0003.
Values sent between devices are 32-bit elements; how exact they have to be, the bound alone decides.
A program may use at most 64 MiB of HBM per device.

v0:
```python
import functools

import jax
import jax.numpy as jnp
from jax import lax
from jax.experimental import pallas as pl
from jax.experimental.pallas import tpu as pltpu
from jax.sharding import PartitionSpec as P

SKETCH = 128
LOW = 16
HIGH = SKETCH // LOW
MESH = pl.DeviceIdType.MESH
epsilon = 1e-06
highest = lax.Precision.HIGHEST
f32 = jnp.float32
bf16 = jnp.bfloat16


def harmonic(first, second):
    return 2.0 * first * second / (first + second)


def total(field):
    return jnp.sum(jnp.sum(field, axis=1, keepdims=True), axis=0, keepdims=True)


def coefficients(s0, s1, s2):
    beta = jnp.sqrt(total(s0 * s0) + epsilon)
    inv_beta = 1.0 / beta
    q0 = s0 * inv_beta
    p0 = s1 * inv_beta
    h00 = total(q0 * p0)
    t0 = p0 - h00 * q0
    n0 = jnp.sqrt(total(t0 * t0) + epsilon)
    inv_n0 = 1.0 / n0
    q1 = t0 * inv_n0
    p1 = (s2 * inv_beta - h00 * p0) * inv_n0
    h01 = total(q0 * p1)
    h11 = total(q1 * p1)
    t1 = p1 - h01 * q0 - h11 * q1
    n1sq = total(t1 * t1) + epsilon
    m00 = h00 * h00 + n0 * n0
    m01 = h00 * h01 + n0 * h11
    m11 = h01 * h01 + h11 * h11 + n1sq
    b0 = beta * h00
    b1 = beta * h01
    l00 = jnp.sqrt(m00)
    l10 = m01 / l00
    l11 = jnp.sqrt(m11 - l10 * l10)
    f0 = b0 / l00
    f1 = (b1 - l10 * f0) / l11
    y1 = f1 / l11
    y0 = (f0 - l10 * y1) / l00
    c1 = y1 * inv_beta * inv_n0
    c0 = y0 * inv_beta - c1 * h00
    return c0, c1


def kernel(
    ngx, ngy, nx, ny, nz,
    f_hbm, w_hbm, m_hbm, s_hbm, d_hbm,
    answer, rest,
    z1, z2, r, w, m, slot, d, cond, cap, lx, ly, lylow, lz, onehot, wh, wl, wh1, wl1, rows,
    hx_r, hx_c, hx_z, hx_s, hx_d, hy_rc, hy_z, hy_s, hy_d, py_rc, py_z, py_s, py_d,
    mine, gathered, load_sem, hs_sem, hr_sem, as_sem, ar_sem, known,
):
    gx = lax.axis_index("gx")
    gy = lax.axis_index("gy")
    count = ngx * ngy
    me = gx * ngy + gy

    loads = [
        pltpu.make_async_copy(src, dst, load_sem.at[i])
        for i, (src, dst) in enumerate(
            ((w_hbm, w), (m_hbm, m), (f_hbm, r), (s_hbm, slot), (d_hbm, d))
        )
    ]
    for load in loads:
        load.start()

    def peer(step):
        other = lax.rem(me + step, count)
        return {"gx": lax.div(other, ngy), "gy": lax.rem(other, ngy)}

    barrier = pltpu.get_barrier_semaphore()

    for step in range(1, ngx):
        other = {"gx": lax.rem(gx + step, ngx), "gy": gy}
        pl.semaphore_signal(barrier, inc=1, device_id=other, device_id_type=MESH)

    has_x = (gx > 0, gx < ngx - 1)
    has_y = (gy > 0, gy < ngy - 1)
    to_x = ({"gx": gx - 1, "gy": gy}, {"gx": gx + 1, "gy": gy})
    to_y = ({"gx": gx, "gy": gy - 1}, {"gx": gx, "gy": gy + 1})
    for s in (0, 1):

        @pl.when(has_y[s])
        def _():
            pl.semaphore_signal(barrier, inc=1, device_id=to_y[s], device_id_type=MESH)

    def tell(turn):
        for s in (0, 1):

            @pl.when(has_y[s])
            def _():
                pl.semaphore_signal(known.at[turn, 1 - s], inc=1, device_id=to_y[s], device_id_type=MESH)

    def hear(turn):
        for s in (0, 1):

            @pl.when(has_y[s])
            def _():
                pl.semaphore_wait(known.at[turn, s], 1)

    edge_x = (0, nx - 1)
    edge_y = (0, ny - 1)

    def remote(src, dst, index, side, target):
        return pltpu.make_async_remote_copy(
            src_ref=src,
            dst_ref=dst.at[1 - side],
            send_sem=hs_sem.at[index, side],
            recv_sem=hr_sem.at[index, 1 - side],
            device_id=target,
            device_id_type=MESH,
        )

    def x_copies(src, dst, index):
        return [(has_x[s], remote(src.at[edge_x[s]], dst, index, s, to_x[s])) for s in (0, 1)]

    def y_copies(src, dst, index):
        return [(has_y[s], remote(src.at[s], dst, index, s, to_y[s])) for s in (0, 1)]

    def begin(copies):
        for there, copy in copies:
            pl.when(there)(copy.start)

    def arrive(copies):
        for there, copy in copies:
            pl.when(there)(copy.wait_send)

    def recv_wait(dst, index, side, src, there, target):
        copy = pltpu.make_async_remote_copy(
            src_ref=src,
            dst_ref=dst.at[side],
            send_sem=hs_sem.at[index, side],
            recv_sem=hr_sem.at[index, side],
            device_id=target,
            device_id_type=MESH,
        )
        pl.when(there)(copy.wait_recv)

    loads[0].wait()
    loads[1].wait()
    for x in range(nx):
        phase = m[x]
        cond[x] = jnp.where(phase == 0, 0.2, jnp.where(phase == 1, 1.0, 0.6)).astype(f32) * (0.5 + w[x])
        cap[x] = jnp.where(phase == 0, 1.0, jnp.where(phase == 1, 2.0, 1.5)).astype(f32)
    loads[2].wait()
    for s in (0, 1):
        for x in range(nx):
            py_rc[s, pl.ds(x, 1), :] = r[x, pl.ds(edge_y[s], 1), :]
            py_rc[s, pl.ds(nx + x, 1), :] = cond[x, pl.ds(edge_y[s], 1), :]

        @pl.when(jnp.logical_not(has_x[s]))
        def _():
            hx_r[s] = jnp.zeros((ny, nz), f32)
            hx_c[s] = jnp.zeros((ny, nz), f32)
            hx_z[s] = jnp.zeros((ny, nz), f32)
            hx_d[s] = jnp.zeros((ny, nz), f32)
            hx_s[s] = jnp.zeros((ny, nz), jnp.int32)

        @pl.when(jnp.logical_not(has_y[s]))
        def _():
            hy_rc[s] = jnp.zeros((2 * nx, nz), f32)
            hy_z[s] = jnp.zeros((nx, nz), f32)
            hy_d[s] = jnp.zeros((nx, nz), f32)
            hy_s[s] = jnp.zeros((nx, nz), jnp.int32)

    pl.semaphore_wait(barrier, ngx - 1 + has_y[0].astype(jnp.int32) + has_y[1].astype(jnp.int32))
    first = x_copies(cond, hx_c, 0) + y_copies(py_rc, hy_rc, 1) + x_copies(r, hx_r, 2)
    begin(first)
    loads[3].wait()
    loads[4].wait()
    for s in (0, 1):
        for x in range(nx):
            py_s[s, pl.ds(x, 1), :] = slot[x, pl.ds(edge_y[s], 1), :]
            py_d[s, pl.ds(x, 1), :] = d[x, pl.ds(edge_y[s], 1), :]
    for x in range(nx):
        rows[x] = slot[x]
    early = x_copies(slot, hx_s, 5) + y_copies(py_s, hy_s, 6) + x_copies(d, hx_d, 7) + y_copies(py_d, hy_d, 8)
    begin(early)
    if ngy > 1:
        tell(1)

    lane = lax.broadcasted_iota(jnp.int32, (ny, nz), 1)
    row = lax.broadcasted_iota(jnp.int32, (ny, nz), 0)
    row_high = lax.broadcasted_iota(jnp.int32, (HIGH, nz), 0)
    row_low = lax.broadcasted_iota(jnp.int32, (LOW, nz), 0)

    def spread(x_ref, x, y, rows):
        return jnp.broadcast_to(x_ref[x, pl.ds(y, 1), :], (rows, nz))

    for x in range(nx):
        here = cond[x]
        if x > 0:
            lx[x] = harmonic(cond[x - 1], here)
        lz[x] = jnp.where(lane == nz - 1, 0.0, harmonic(here, pltpu.roll(here, nz - 1, 1)))

    def build(x, carry):
        for y in range(ny):
            slots = spread(rows, x, y, LOW)
            low = jnp.bitwise_and(slots, LOW - 1)
            onehot[x, y] = jnp.where(low == row_low, 1.0, 0.0).astype(bf16)
        return carry

    lax.fori_loop(0, nx, build, 0)

    def split(x, weighted):
        upper = weighted.astype(bf16).astype(f32)
        wh[x] = upper
        wl[x] = weighted - upper

    def adder(parts):
        def add(x, sums):
            for y in range(ny):
                mask = lax.shift_right_logical(spread(rows, x, y, HIGH), 4) == row_high
                left = jnp.concatenate(
                    [jnp.where(mask, spread(part, x, y, HIGH), 0.0) for part in parts], axis=0
                ).astype(bf16)
                sums = sums + lax.dot_general(
                    left, onehot[x, y], (((1,), (1,)), ((), ())), preferred_element_type=f32
                )
            return sums

        return add

    def finish(sums):
        both = sums[:HIGH] + sums[HIGH:]
        lanes = lax.broadcasted_iota(jnp.int32, (LOW, SKETCH), 1)
        expand = jnp.where(
            jnp.bitwise_and(lanes, LOW - 1) == lax.broadcasted_iota(jnp.int32, (LOW, SKETCH), 0), 1.0, 0.0
        ).astype(f32)
        wide = jnp.dot(both, expand, precision=highest, preferred_element_type=f32)
        keep = lax.shift_right_logical(
            lax.broadcasted_iota(jnp.int32, (HIGH, SKETCH), 1), 4
        ) == lax.broadcasted_iota(jnp.int32, (HIGH, SKETCH), 0)
        return jnp.sum(jnp.where(keep, wide, 0.0), axis=0, keepdims=True)

    def apply(field, halo_x, halo_y, out):
        for x in range(nx):
            v = field[x]
            if x == 0:
                low = v if halo_x is None else v - halo_x[0]
            else:
                low = v - field[x - 1]
            if x == nx - 1:
                top = v if halo_x is None else v - halo_x[1]
            else:
                top = v - field[x + 1]
            acc = cap[x] * v + lx[x + 1] * top + lx[x] * low
            first_row, last_row = (0.0, 0.0) if halo_y is None else (halo_y(0, x), halo_y(1, x))
            up = jnp.where(row == ny - 1, last_row, pltpu.roll(v, ny - 1, 0))
            flux = ly[x] * (v - up)
            entering = lylow[pl.ds(x, 1), :] * (first_row - v[0:1, :])
            acc = acc + flux - jnp.where(row == 0, entering, pltpu.roll(flux, 1, 0))
            flux = lz[x] * (v - pltpu.roll(v, nz - 1, 1))
            out[x] = acc + flux - pltpu.roll(flux, 1, 1)

    mine[3:4, :] = jnp.zeros((1, SKETCH), f32)
    for x in range(nx):
        split(x, d[x] * r[x])
    mine[0:1, :] = finish(lax.fori_loop(0, nx, adder((wh, wl)), jnp.zeros((2 * HIGH, LOW), f32)))
    if ngy > 2:
        hear(1)
        tell(2)

    for s in (0, 1):
        recv_wait(hx_c, 0, s, cond.at[0], has_x[s], to_x[s])
        recv_wait(hy_rc, 1, s, py_rc.at[0], has_y[s], to_y[s])
        recv_wait(hx_r, 2, s, r.at[0], has_x[s], to_x[s])
    lx[0] = harmonic(hx_c[0], cond[0])
    lx[nx] = harmonic(cond[nx - 1], hx_c[1])
    for x in range(nx):
        here = cond[x]
        up = jnp.where(row == ny - 1, hy_rc[1, pl.ds(nx + x, 1), :], pltpu.roll(here, ny - 1, 0))
        ly[x] = harmonic(here, up)
        lylow[pl.ds(x, 1), :] = harmonic(hy_rc[0, pl.ds(nx + x, 1), :], here[0:1, :])
    apply(r, hx_r, lambda s, x: hy_rc[s, pl.ds(x, 1), :], z1)
    for s in (0, 1):
        for x in range(nx):
            py_z[s, pl.ds(x, 1), :] = z1[x, pl.ds(edge_y[s], 1), :]
    second = x_copies(z1, hx_z, 3) + y_copies(py_z, hy_z, 4)
    begin(second)
    for turn in range(3, ngy):
        hear(turn - 1)
        tell(turn)
    apply(z1, None, None, z2)
    for x in range(nx):
        weighted = d[x] * z1[x]
        upper = weighted.astype(bf16).astype(f32)
        wh1[x] = upper
        wl1[x] = weighted - upper
        split(x, d[x] * z2[x])
    sums = lax.fori_loop(0, nx, adder((wh1, wl1, wh, wl)), jnp.zeros((4 * HIGH, LOW), f32))
    for s in (0, 1):
        recv_wait(hx_s, 5, s, slot.at[0], has_x[s], to_x[s])
        recv_wait(hy_s, 6, s, py_s.at[0], has_y[s], to_y[s])
        recv_wait(hx_d, 7, s, d.at[0], has_x[s], to_x[s])
        recv_wait(hy_d, 8, s, py_d.at[0], has_y[s], to_y[s])
        rows[nx + s] = hx_s[s]
        split(nx + s, -lx[nx * s] * z1[edge_x[s]] * hx_d[s])
        edge = []
        for x in range(nx):
            link = lylow[pl.ds(x, 1), :] if s == 0 else ly[x, pl.ds(ny - 1, 1), :]
            edge.append(-link * z1[x, pl.ds(edge_y[s], 1), :] * hy_d[s, pl.ds(x, 1), :])
            rows[nx + 2, pl.ds(s * nx + x, 1), :] = hy_s[s, pl.ds(x, 1), :]
        edge = jnp.concatenate(edge, axis=0)
        upper = edge.astype(bf16).astype(f32)
        wh[nx + 2, pl.ds(s * nx, nx), :] = upper
        wl[nx + 2, pl.ds(s * nx, nx), :] = edge - upper
    for y in range(2 * nx, ny):
        rows[nx + 2, pl.ds(y, 1), :] = jnp.zeros((1, nz), jnp.int32)
        wh[nx + 2, pl.ds(y, 1), :] = jnp.zeros((1, nz), f32)
        wl[nx + 2, pl.ds(y, 1), :] = jnp.zeros((1, nz), f32)
    lax.fori_loop(nx, nx + 3, build, 0)
    halo_sums = lax.fori_loop(nx, nx + 3, adder((wh, wl)), jnp.zeros((2 * HIGH, LOW), f32))
    mine[1:2, :] = finish(sums[: 2 * HIGH])
    mine[2:3, :] = finish(sums[2 * HIGH :] + halo_sums)

    def share(step, carry):
        pltpu.make_async_remote_copy(
            src_ref=mine,
            dst_ref=gathered.at[me],
            send_sem=as_sem.at[step],
            recv_sem=ar_sem.at[me],
            device_id=peer(step),
            device_id_type=MESH,
        ).start()
        return carry

    if ngy > 1:
        hear(ngy - 1)
    lax.fori_loop(1, count, share, 0)
    gathered[me] = mine[...]
    arrive(first)
    arrive(early)
    arrive(second)
    for s in (0, 1):
        recv_wait(hx_z, 3, s, z1.at[0], has_x[s], to_x[s])
        recv_wait(hy_z, 4, s, py_z.at[0], has_y[s], to_y[s])
        z2[edge_x[s]] = z2[edge_x[s]] - lx[nx * s] * hx_z[s]
        for x in range(nx):
            link = lylow[pl.ds(x, 1), :] if s == 0 else ly[x, pl.ds(ny - 1, 1), :]
            at = (x, pl.ds(edge_y[s], 1), slice(None))
            z2[at] = z2[at] - link * hy_z[s, pl.ds(x, 1), :]

    def collect(step, carry):
        other = lax.rem(me + step, count)
        copy = pltpu.make_async_remote_copy(
            src_ref=mine,
            dst_ref=gathered.at[other],
            send_sem=as_sem.at[step],
            recv_sem=ar_sem.at[other],
            device_id=peer(step),
            device_id_type=MESH,
        )
        copy.wait_recv()
        copy.wait_send()
        return carry

    lax.fori_loop(1, count, collect, 0)
    summed = jnp.sum(gathered[...], axis=0)
    c0, c1 = coefficients(summed[0:1], summed[1:2], summed[2:3])
    for x in range(nx):
        answer[x] = c0 * r[x] + c1 * z1[x]
        rest[x] = r[x] - c0 * z1[x] - c1 * z2[x]


def put_out(answer, rest, answer_out, rest_out, sem):
    one = pltpu.make_async_copy(answer, answer_out, sem.at[0])
    two = pltpu.make_async_copy(rest, rest_out, sem.at[1])
    one.start()
    two.start()
    one.wait()
    two.wait()


def body(ngx, ngy, f, w, m, s, d):
    nx, ny, nz = f.shape
    count = ngx * ngy
    vm = lambda shape, dtype=f32: pltpu.VMEM(shape, dtype)
    block = (nx, ny, nz)
    wide = (nx + 3, ny, nz)
    assert 2 * nx <= ny
    answer, rest = pl.pallas_call(
        functools.partial(kernel, ngx, ngy, nx, ny, nz),
        out_shape=(vm(block), vm(block)),
        in_specs=[pl.BlockSpec(memory_space=pl.ANY)] * 5,
        out_specs=[pl.BlockSpec(memory_space=pltpu.VMEM)] * 2,
        scratch_shapes=[
            vm(block), vm(block),
            vm(block), vm(block), vm(block, jnp.int32), vm(block, jnp.int32), vm(block),
            vm(block), vm(block),
            vm((nx + 1, ny, nz)), vm(block), vm((nx, nz)), vm(block),
            vm((nx + 3, ny, LOW, nz), bf16), vm(wide), vm(wide), vm(block), vm(block), vm(wide, jnp.int32),
            vm((2, ny, nz)), vm((2, ny, nz)), vm((2, ny, nz)), vm((2, ny, nz), jnp.int32), vm((2, ny, nz)),
            vm((2, 2 * nx, nz)), vm((2, nx, nz)), vm((2, nx, nz), jnp.int32), vm((2, nx, nz)),
            vm((2, 2 * nx, nz)), vm((2, nx, nz)), vm((2, nx, nz), jnp.int32), vm((2, nx, nz)),
            vm((4, SKETCH)), vm((count, 4, SKETCH)),
            pltpu.SemaphoreType.DMA((5,)),
            pltpu.SemaphoreType.DMA((9, 2)),
            pltpu.SemaphoreType.DMA((9, 2)),
            pltpu.SemaphoreType.DMA((count,)),
            pltpu.SemaphoreType.DMA((count,)),
            pltpu.SemaphoreType.REGULAR((ngy, 2)),
        ],
        compiler_params=pltpu.CompilerParams(collective_id=0, has_side_effects=True),
        name="sketched_gmres",
    )(f, w, m, s, d)
    return pl.pallas_call(
        put_out,
        out_shape=(jax.ShapeDtypeStruct(block, f32), jax.ShapeDtypeStruct(block, f32)),
        in_specs=[pl.BlockSpec(memory_space=pltpu.VMEM)] * 2,
        out_specs=[pl.BlockSpec(memory_space=pl.ANY)] * 2,
        scratch_shapes=[pltpu.SemaphoreType.DMA((2,))],
        name="put_out",
    )(pltpu.with_memory_space_constraint(answer, pltpu.VMEM), pltpu.with_memory_space_constraint(rest, pltpu.VMEM))


def solution(mesh):
    spec = P(("parts", "gx"), "gy", None)
    return jax.shard_map(
        functools.partial(body, mesh.shape["gx"], mesh.shape["gy"]),
        mesh=mesh,
        in_specs=(spec,) * 5,
        out_specs=(spec, spec),
        check_vma=False,
    )
```

profile of v0, /device:TPU:0, one launch (start us, length us, event | category | flops | bytes accessed | tf_op | source)
XLA Modules:
  0.0 17.0 jit_solution(8216243121625963552)
XLA Ops:
  0.6 15.7 %sketched_gmres.1 = (f32[4,8,1024]{2,1,0:T(8,128)S(1)}, f32[4,8,1024]{2,1,0:T(8,128)S(1)}) custom-call(f32[4,8,1024]{2,1,0:T(8,128)} %f_hbm.1, f32[4,8,1024]{2,1,0:T(8,128)} %w_hbm.1, s32[4,8,1024]{2,1,0:T(8,128)} %m_hbm.1, s32[4,8,1024]{2,1,0:T(8,128)} %s_hbm.1, f32[4,8,1024]{2,1,0:T(8,128)} %d_hbm.1), custom_call_target="tpu_custom_call" | custom-call | tf_op jit(solution)/shard_map/sketched_gmres/pallas_call | solution.py:397
  16.3 0.7 %put_out.1 = (f32[4,8,1024]{2,1,0:T(8,128)}, f32[4,8,1024]{2,1,0:T(8,128)}) custom-call(f32[4,8,1024]{2,1,0:T(8,128)S(1)} %get-tuple-element.4.answer, f32[4,8,1024]{2,1,0:T(8,128)S(1)} %get-tuple-element.5.rest), custom_call_target="tpu_custom_call" | custom-call | tf_op jit(solution)/shard_map/put_out/pallas_call | solution.py:422
where the time goes:
time: 17.2 us; the launch traced here: 17 us
  Pallas kernels  16.4 us (95%)
  between operations  0.64 us (4%)
    pallas_call x1, Pallas kernels, body(): pl.pallas_call(functools.partial(kernel, ngx, ngy, nx, ny, nz), out_shape...  15.7 us
    pallas_call x1, Pallas kernels, body(): pl.pallas_call(put_out, out_shape=(jax.ShapeDtypeStruct(block, f32), jax....  0.72 us

commit v1 on v0

v1 whole, which is shorter than its diff:
```python
import functools

import jax
import jax.numpy as jnp
from jax import lax
from jax.experimental import pallas as pl
from jax.experimental.pallas import tpu as pltpu
from jax.sharding import PartitionSpec as P

SKETCH = 128
LOW = 16
HIGH = SKETCH // LOW
MESH = pl.DeviceIdType.MESH
epsilon = 1e-06
highest = lax.Precision.HIGHEST
f32 = jnp.float32
bf16 = jnp.bfloat16


def harmonic(first, second):
    return 2.0 * first * second / (first + second)


def total(field):
    return jnp.sum(jnp.sum(field, axis=1, keepdims=True), axis=0, keepdims=True)


def coefficients(s0, s1, s2):
    beta2 = total(s0 * s0) + epsilon
    h00 = total(s0 * s1) / beta2
    t0 = s1 - h00 * s0
    w1 = s2 - h00 * s1
    n0sq = total(t0 * t0) / beta2 + epsilon
    in_q0 = total(s0 * w1) / beta2
    h11 = total(t0 * w1) / (beta2 * n0sq)
    n0 = jnp.sqrt(n0sq)
    h01 = in_q0 / n0
    t1 = w1 - in_q0 * s0 - h11 * t0
    n1sq = total(t1 * t1) / (beta2 * n0sq) + epsilon
    m00 = h00 * h00 + n0sq
    m01 = h00 * h01 + n0 * h11
    m11 = h01 * h01 + h11 * h11 + n1sq
    l00 = jnp.sqrt(m00)
    l10 = m01 / l00
    l11 = jnp.sqrt(m11 - l10 * l10)
    f0 = h00 / l00
    f1 = (h01 - l10 * f0) / l11
    y1 = f1 / l11
    y0 = (f0 - l10 * y1) / l00
    c1 = y1 / n0
    c0 = y0 - c1 * h00
    return c0, c1


def kernel(
    ngx, ngy, nx, ny, nz,
    f_hbm, w_hbm, m_hbm, s_hbm, d_hbm,
    answer, rest,
    z1, z2, r, w, m, slot, d, cond, diag, lx, ly, lydown, lz, lzleft, lyb, onehot, parts, wedge, sedge,
    hx_r, hx_c, hx_z, hx_s, hx_d, hy_rc, hy_z, hy_s, hy_d, py_rc, py_z, py_s, py_d,
    mine, gathered, load_sem, hs_sem, hr_sem, as_sem, ar_sem, known,
):
    gx = lax.axis_index("gx")
    gy = lax.axis_index("gy")
    count = ngx * ngy
    me = gx * ngy + gy


    def peer(step):
        other = lax.rem(me + step, count)
        return {"gx": lax.div(other, ngy), "gy": lax.rem(other, ngy)}

    barrier = pltpu.get_barrier_semaphore()

    for step in range(1, ngx):
        other = {"gx": lax.rem(gx + step, ngx), "gy": gy}
        pl.semaphore_signal(barrier, inc=1, device_id=other, device_id_type=MESH)

    has_x = (gx > 0, gx < ngx - 1)
    has_y = (gy > 0, gy < ngy - 1)
    to_x = ({"gx": gx - 1, "gy": gy}, {"gx": gx + 1, "gy": gy})
    to_y = ({"gx": gx, "gy": gy - 1}, {"gx": gx, "gy": gy + 1})
    for s in (0, 1):

        @pl.when(has_y[s])
        def _():
            pl.semaphore_signal(barrier, inc=1, device_id=to_y[s], device_id_type=MESH)

    loads = [
        pltpu.make_async_copy(src, dst, load_sem.at[i])
        for i, (src, dst) in enumerate(
            ((w_hbm, w), (m_hbm, m), (f_hbm, r), (s_hbm, slot), (d_hbm, d))
        )
    ]
    for load in loads:
        load.start()

    def tell(turn):
        for s in (0, 1):

            @pl.when(has_y[s])
            def _():
                pl.semaphore_signal(known.at[turn, 1 - s], inc=1, device_id=to_y[s], device_id_type=MESH)

    def hear(turn):
        for s in (0, 1):

            @pl.when(has_y[s])
            def _():
                pl.semaphore_wait(known.at[turn, s], 1)

    edge_x = (0, nx - 1)
    edge_y = (0, ny - 1)

    def remote(src, dst, index, side, target):
        return pltpu.make_async_remote_copy(
            src_ref=src,
            dst_ref=dst.at[1 - side],
            send_sem=hs_sem.at[index, side],
            recv_sem=hr_sem.at[index, 1 - side],
            device_id=target,
            device_id_type=MESH,
        )

    def x_copies(src, dst, index):
        return [(has_x[s], remote(src.at[edge_x[s]], dst, index, s, to_x[s])) for s in (0, 1)]

    def y_copies(src, dst, index):
        return [(has_y[s], remote(src.at[s], dst, index, s, to_y[s])) for s in (0, 1)]

    def begin(copies):
        for there, copy in copies:
            pl.when(there)(copy.start)

    def arrive(copies):
        for there, copy in copies:
            pl.when(there)(copy.wait_send)

    def recv_wait(dst, index, side, src, there, target):
        copy = pltpu.make_async_remote_copy(
            src_ref=src,
            dst_ref=dst.at[side],
            send_sem=hs_sem.at[index, side],
            recv_sem=hr_sem.at[index, side],
            device_id=target,
            device_id_type=MESH,
        )
        pl.when(there)(copy.wait_recv)

    loads[0].wait()
    loads[1].wait()
    for x in range(nx):
        phase = m[x]
        cond[x] = jnp.where(phase == 0, 0.2, jnp.where(phase == 1, 1.0, 0.6)).astype(f32) * (0.5 + w[x])
    loads[2].wait()
    for s in (0, 1):
        for x in range(nx):
            py_rc[s, pl.ds(x, 1), :] = r[x, pl.ds(edge_y[s], 1), :]
            py_rc[s, pl.ds(nx + x, 1), :] = cond[x, pl.ds(edge_y[s], 1), :]

        @pl.when(jnp.logical_not(has_x[s]))
        def _():
            hx_r[s] = jnp.zeros((ny, nz), f32)
            hx_c[s] = jnp.zeros((ny, nz), f32)
            hx_z[s] = jnp.zeros((ny, nz), f32)
            hx_d[s] = jnp.zeros((ny, nz), f32)
            hx_s[s] = jnp.zeros((ny, nz), jnp.int32)

        @pl.when(jnp.logical_not(has_y[s]))
        def _():
            hy_rc[s] = jnp.zeros((2 * nx, nz), f32)
            hy_z[s] = jnp.zeros((nx, nz), f32)
            hy_d[s] = jnp.zeros((nx, nz), f32)
            hy_s[s] = jnp.zeros((nx, nz), jnp.int32)

    pl.semaphore_wait(barrier, ngx - 1 + has_y[0].astype(jnp.int32) + has_y[1].astype(jnp.int32))
    first = x_copies(cond, hx_c, 0) + y_copies(py_rc, hy_rc, 1) + x_copies(r, hx_r, 2)
    begin(first)
    if ngy > 1:
        tell(1)
    loads[3].wait()
    loads[4].wait()
    for s in (0, 1):
        for x in range(nx):
            py_s[s, pl.ds(x, 1), :] = slot[x, pl.ds(edge_y[s], 1), :]
            py_d[s, pl.ds(x, 1), :] = d[x, pl.ds(edge_y[s], 1), :]
    early = x_copies(slot, hx_s, 5) + y_copies(py_s, hy_s, 6) + x_copies(d, hx_d, 7) + y_copies(py_d, hy_d, 8)
    begin(early)

    lane = lax.broadcasted_iota(jnp.int32, (ny, nz), 1)
    row = lax.broadcasted_iota(jnp.int32, (ny, nz), 0)
    row_high = lax.broadcasted_iota(jnp.int32, (HIGH, nz), 0)
    row_low = lax.broadcasted_iota(jnp.int32, (LOW, nz), 0)

    def spread(ref, y, rows):
        return jnp.broadcast_to(ref[pl.ds(y, 1), :], (rows, nz))

    def low_rows(slots, y):
        low = jnp.bitwise_and(spread(slots, y, LOW), LOW - 1)
        return jnp.where(low == row_low, 1.0, 0.0).astype(bf16)

    def add_row(sums, slots, fields, right, y):
        mask = lax.shift_right_logical(spread(slots, y, HIGH), 4) == row_high
        left = jnp.concatenate([jnp.where(mask, spread(field, y, HIGH), 0.0) for field in fields], axis=0)
        return sums + lax.dot_general(
            left.astype(bf16), right, (((1,), (1,)), ((), ())), preferred_element_type=f32
        )

    def split(high, low, weighted):
        upper = weighted.astype(bf16).astype(f32)
        high[...] = upper
        low[...] = weighted - upper

    for x in range(nx):
        here = cond[x]
        if x > 0:
            lx[x] = harmonic(cond[x - 1], here)
        right = jnp.where(lane == nz - 1, 0.0, harmonic(here, pltpu.roll(here, nz - 1, 1)))
        up = jnp.where(row == ny - 1, 0.0, harmonic(here, pltpu.roll(here, ny - 1, 0)))
        lz[x] = right
        lzleft[x] = pltpu.roll(right, 1, 1)
        ly[x] = up
        lydown[x] = pltpu.roll(up, 1, 0)
    for x in range(nx):
        phase = m[x]
        cap = jnp.where(phase == 0, 1.0, jnp.where(phase == 1, 2.0, 1.5)).astype(f32)
        whole = cap + lz[x] + lzleft[x] + ly[x] + lydown[x]
        if x > 0:
            whole = whole + lx[x]
        if x < nx - 1:
            whole = whole + lx[x + 1]
        diag[x] = whole

    def apply(field, x):
        v = field[x]
        out = diag[x] * v
        if x > 0:
            out = out - lx[x] * field[x - 1]
        if x < nx - 1:
            out = out - lx[x + 1] * field[x + 1]
        out = out - ly[x] * pltpu.roll(v, ny - 1, 0) - lydown[x] * pltpu.roll(v, 1, 0)
        return out - lz[x] * pltpu.roll(v, nz - 1, 1) - lzleft[x] * pltpu.roll(v, 1, 1)

    for x in range(nx):
        z1[x] = apply(r, x)

    def begin_sketch(x, sums):
        split(parts.at[0, x], parts.at[1, x], d[x] * r[x])
        for y in range(ny):
            right = low_rows(slot.at[x], y)
            onehot[x, y] = right
            sums = add_row(sums, slot.at[x], (parts.at[0, x], parts.at[1, x]), right, y)
        return sums

    sums = lax.fori_loop(0, nx, begin_sketch, jnp.zeros((2 * HIGH, LOW), f32))
    mine[...] = jnp.zeros((HIGH, SKETCH), f32)
    mine[:, 0:LOW] = sums[:HIGH] + sums[HIGH:]
    for turn in range(2, ngy):
        hear(turn - 1)
        tell(turn)

    for s in (0, 1):
        recv_wait(hx_c, 0, s, cond.at[0], has_x[s], to_x[s])
        recv_wait(hy_rc, 1, s, py_rc.at[0], has_y[s], to_y[s])
        recv_wait(hx_r, 2, s, r.at[0], has_x[s], to_x[s])
    for s in (0, 1):
        e = edge_x[s]
        link = harmonic(hx_c[s], cond[e])
        lx[nx * s] = link
        z1[e] = z1[e] + link * (r[e] - hx_r[s])
    for s in (0, 1):
        for x in range(nx):
            link = harmonic(hy_rc[s, pl.ds(nx + x, 1), :], py_rc[s, pl.ds(nx + x, 1), :])
            lyb[s, pl.ds(x, 1), :] = link
            flux = link * (py_rc[s, pl.ds(x, 1), :] - hy_rc[s, pl.ds(x, 1), :])
            after = z1[x, pl.ds(edge_y[s], 1), :] + flux
            z1[x, pl.ds(edge_y[s], 1), :] = after
            py_z[s, pl.ds(x, 1), :] = after
    second = x_copies(z1, hx_z, 3) + y_copies(py_z, hy_z, 4)
    begin(second)
    for x in range(nx):
        out = apply(z1, x)
        for s in (0, 1):
            if x == edge_x[s]:
                out = out + lx[nx * s] * z1[x]
        z2[x] = out
        for s in (0, 1):
            at = (x, pl.ds(edge_y[s], 1), slice(None))
            z2[at] = z2[at] + lyb[s, pl.ds(x, 1), :] * py_z[s, pl.ds(x, 1), :]
    sums = jnp.zeros((4 * HIGH, LOW), f32)
    for x in range(nx):
        split(parts.at[0, x], parts.at[1, x], d[x] * z1[x])
        split(parts.at[2, x], parts.at[3, x], d[x] * z2[x])
        for y in range(ny):
            sums = add_row(sums, slot.at[x], [parts.at[k, x] for k in range(4)], onehot[x, y], y)
    for s in (0, 1):
        recv_wait(hx_s, 5, s, slot.at[0], has_x[s], to_x[s])
        recv_wait(hy_s, 6, s, py_s.at[0], has_y[s], to_y[s])
        recv_wait(hx_d, 7, s, d.at[0], has_x[s], to_x[s])
        recv_wait(hy_d, 8, s, py_d.at[0], has_y[s], to_y[s])
    edge_sums = jnp.zeros((2 * HIGH, LOW), f32)
    for s in (0, 1):
        split(wedge.at[0, s], wedge.at[1, s], -lx[nx * s] * z1[edge_x[s]] * hx_d[s])
        for x in range(nx):
            at = pl.ds(s * nx + x, 1)
            edge = -lyb[s, pl.ds(x, 1), :] * py_z[s, pl.ds(x, 1), :] * hy_d[s, pl.ds(x, 1), :]
            upper = edge.astype(bf16).astype(f32)
            wedge[0, 2, at, :] = upper
            wedge[1, 2, at, :] = edge - upper
            sedge[at, :] = hy_s[s, pl.ds(x, 1), :]
    for t, slots in enumerate((hx_s.at[0], hx_s.at[1], sedge)):
        for y in range(ny if t < 2 else 2 * nx):
            edge_sums = add_row(edge_sums, slots, (wedge.at[0, t], wedge.at[1, t]), low_rows(slots, y), y)
    mine[:, LOW : 2 * LOW] = sums[:HIGH] + sums[HIGH : 2 * HIGH]
    mine[:, 2 * LOW : 3 * LOW] = (
        sums[2 * HIGH : 3 * HIGH] + sums[3 * HIGH :] + edge_sums[:HIGH] + edge_sums[HIGH:]
    )

    def share(step, carry):
        pltpu.make_async_remote_copy(
            src_ref=mine,
            dst_ref=gathered.at[me],
            send_sem=as_sem.at[step],
            recv_sem=ar_sem.at[me],
            device_id=peer(step),
            device_id_type=MESH,
        ).start()
        return carry

    if ngy > 1:
        hear(ngy - 1)
    lax.fori_loop(1, count, share, 0)
    gathered[me] = mine[...]
    arrive(first)
    arrive(early)
    arrive(second)
    for s in (0, 1):
        recv_wait(hx_z, 3, s, z1.at[0], has_x[s], to_x[s])
        recv_wait(hy_z, 4, s, py_z.at[0], has_y[s], to_y[s])
        z2[edge_x[s]] = z2[edge_x[s]] - lx[nx * s] * hx_z[s]
        for x in range(nx):
            link = lyb[s, pl.ds(x, 1), :]
            at = (x, pl.ds(edge_y[s], 1), slice(None))
            z2[at] = z2[at] - link * hy_z[s, pl.ds(x, 1), :]

    def collect(step, carry):
        other = lax.rem(me + step, count)
        copy = pltpu.make_async_remote_copy(
            src_ref=mine,
            dst_ref=gathered.at[other],
            send_sem=as_sem.at[step],
            recv_sem=ar_sem.at[other],
            device_id=peer(step),
            device_id_type=MESH,
        )
        copy.wait_recv()
        copy.wait_send()
        return carry

    lax.fori_loop(1, count, collect, 0)
    summed = jnp.sum(gathered[...], axis=0)
    c0, c1 = coefficients(*(summed[:, k * LOW : (k + 1) * LOW] for k in range(3)))
    for x in range(nx):
        answer[x] = c0 * r[x] + c1 * z1[x]
        rest[x] = r[x] - c0 * z1[x] - c1 * z2[x]


def put_out(answer, rest, answer_out, rest_out, sem):
    one = pltpu.make_async_copy(answer, answer_out, sem.at[0])
    two = pltpu.make_async_copy(rest, rest_out, sem.at[1])
    one.start()
    two.start()
    one.wait()
    two.wait()


def body(ngx, ngy, f, w, m, s, d):
    nx, ny, nz = f.shape
    count = ngx * ngy
    vm = lambda shape, dtype=f32: pltpu.VMEM(shape, dtype)
    block = (nx, ny, nz)
    assert 2 * nx <= ny
    answer, rest = pl.pallas_call(
        functools.partial(kernel, ngx, ngy, nx, ny, nz),
        out_shape=(vm(block), vm(block)),
        in_specs=[pl.BlockSpec(memory_space=pl.ANY)] * 5,
        out_specs=[pl.BlockSpec(memory_space=pltpu.VMEM)] * 2,
        scratch_shapes=[
            vm(block), vm(block),
            vm(block), vm(block), vm(block, jnp.int32), vm(block, jnp.int32), vm(block),
            vm(block), vm(block),
            vm((nx + 1, ny, nz)), vm(block), vm(block), vm(block), vm(block), vm((2, nx, nz)),
            vm((nx, ny, LOW, nz), bf16), vm((4, nx, ny, nz)), vm((2, 3, ny, nz)), vm((ny, nz), jnp.int32),
            vm((2, ny, nz)), vm((2, ny, nz)), vm((2, ny, nz)), vm((2, ny, nz), jnp.int32), vm((2, ny, nz)),
            vm((2, 2 * nx, nz)), vm((2, nx, nz)), vm((2, nx, nz), jnp.int32), vm((2, nx, nz)),
            vm((2, 2 * nx, nz)), vm((2, nx, nz)), vm((2, nx, nz), jnp.int32), vm((2, nx, nz)),
            vm((HIGH, SKETCH)), vm((count, HIGH, SKETCH)),
            pltpu.SemaphoreType.DMA((5,)),
            pltpu.SemaphoreType.DMA((9, 2)),
            pltpu.SemaphoreType.DMA((9, 2)),
            pltpu.SemaphoreType.DMA((count,)),
            pltpu.SemaphoreType.DMA((count,)),
            pltpu.SemaphoreType.REGULAR((ngy, 2)),
        ],
        compiler_params=pltpu.CompilerParams(collective_id=0, has_side_effects=True),
        name="sketched_gmres",
    )(f, w, m, s, d)
    return pl.pallas_call(
        put_out,
        out_shape=(jax.ShapeDtypeStruct(block, f32), jax.ShapeDtypeStruct(block, f32)),
        in_specs=[pl.BlockSpec(memory_space=pltpu.VMEM)] * 2,
        out_specs=[pl.BlockSpec(memory_space=pl.ANY)] * 2,
        scratch_shapes=[pltpu.SemaphoreType.DMA((2,))],
        name="put_out",
    )(pltpu.with_memory_space_constraint(answer, pltpu.VMEM), pltpu.with_memory_space_constraint(rest, pltpu.VMEM))


def solution(mesh):
    spec = P(("parts", "gx"), "gy", None)
    return jax.shard_map(
        functools.partial(body, mesh.shape["gx"], mesh.shape["gy"]),
        mesh=mesh,
        in_specs=(spec,) * 5,
        out_specs=(spec, spec),
        check_vma=False,
    )
```

time: 17.2 us -> 16.6 us (0.965)
  Pallas kernels: 16.4 us -> 15.8 us
    pallas_call x1, Pallas kernels: 15.7 us -> 15.1 us  [body(): pl.pallas_call(functools.partial(kernel, ngx, ngy, nx, ny, nz), out_shape...]
where the time goes in v1:
time: 16.6 us; the launch traced here: 16.4 us
  Pallas kernels  15.8 us (95%)
  between operations  0.64 us (4%)
    pallas_call x1, Pallas kernels, body(): pl.pallas_call(functools.partial(kernel, ngx, ngy, nx, ny, nz), out_shape...  15.1 us
    pallas_call x1, Pallas kernels, body(): pl.pallas_call(put_out, out_shape=(jax.ShapeDtypeStruct(block, f32), jax....  0.72 us

profile of v1, /device:TPU:0, one launch (start us, length us, event | category | flops | bytes accessed | tf_op | source)
XLA Modules:
  0.0 16.4 jit_solution(15474882754338089659)
XLA Ops:
  0.6 15.1 %sketched_gmres.1 = (f32[4,8,1024]{2,1,0:T(8,128)S(1)}, f32[4,8,1024]{2,1,0:T(8,128)S(1)}) custom-call(f32[4,8,1024]{2,1,0:T(8,128)} %f_hbm.1, f32[4,8,1024]{2,1,0:T(8,128)} %w_hbm.1, s32[4,8,1024]{2,1,0:T(8,128)} %m_hbm.1, s32[4,8,1024]{2,1,0:T(8,128)} %s_hbm.1, f32[4,8,1024]{2,1,0:T(8,128)} %d_hbm.1), custom_call_target="tpu_custom_call" | custom-call | tf_op jit(solution)/shard_map/sketched_gmres/pallas_call | solution.py:383
  15.7 0.7 %put_out.1 = (f32[4,8,1024]{2,1,0:T(8,128)}, f32[4,8,1024]{2,1,0:T(8,128)}) custom-call(f32[4,8,1024]{2,1,0:T(8,128)S(1)} %get-tuple-element.4.answer, f32[4,8,1024]{2,1,0:T(8,128)S(1)} %get-tuple-element.5.rest), custom_call_target="tpu_custom_call" | custom-call | tf_op jit(solution)/shard_map/put_out/pallas_call | solution.py:408

commit v2 on v1

v2 whole, which is shorter than its diff:
```python
import functools

import jax
import jax.numpy as jnp
from jax import lax
from jax.experimental import pallas as pl
from jax.experimental.pallas import tpu as pltpu
from jax.sharding import PartitionSpec as P

SKETCH = 128
LOW = 16
HIGH = SKETCH // LOW
MESH = pl.DeviceIdType.MESH
epsilon = 1e-06
highest = lax.Precision.HIGHEST
f32 = jnp.float32
bf16 = jnp.bfloat16


def harmonic(first, second):
    return 2.0 * first * second / (first + second)


def total(field):
    return jnp.sum(jnp.sum(field, axis=1, keepdims=True), axis=0, keepdims=True)


def coefficients(s0, s1, s2):
    inv_beta2 = 1.0 / (total(s0 * s0) + epsilon)
    h00 = total(s0 * s1) * inv_beta2
    t0 = s1 - h00 * s0
    w1 = s2 - h00 * s1
    n0sq = total(t0 * t0) * inv_beta2 + epsilon
    cross = total(s0 * w1) * inv_beta2
    inv_n0sq = 1.0 / n0sq
    h11 = total(t0 * w1) * inv_beta2 * inv_n0sq
    t1 = w1 - cross * s0 - h11 * t0
    n1sq = total(t1 * t1) * inv_beta2 * inv_n0sq + epsilon
    minor = h00 * h11 - cross
    inv_det = 1.0 / (minor * minor + n1sq * (h00 * h00 + n0sq))
    return (minor * (h11 + h00) + h00 * n1sq) * inv_det, -minor * inv_det


def kernel(
    ngx, ngy, nx, ny, nz,
    f_hbm, w_hbm, m_hbm, s_hbm, d_hbm,
    answer, rest,
    z1, z2, r, w, m, slot, d, cond, diag, lx, ly, lydown, lz, lzleft, lyb, onehot, parts, wedge, sedge,
    hx_first, hx_early, hx_z, hy_first, hy_early, hy_z,
    px_first, px_early, py_first, py_early, py_z,
    bulk_x, bulk_y, mine, gathered, load_sem, sent, landed, share_sem, known,
):
    gx = lax.axis_index("gx")
    gy = lax.axis_index("gy")
    count = ngx * ngy
    me = gx * ngy + gy


    def peer(step):
        other = lax.rem(me + step, count)
        return {"gx": lax.div(other, ngy), "gy": lax.rem(other, ngy)}

    barrier = pltpu.get_barrier_semaphore()

    for step in range(1, ngx):
        other = {"gx": lax.rem(gx + step, ngx), "gy": gy}
        pl.semaphore_signal(barrier, inc=1, device_id=other, device_id_type=MESH)

    has_x = (gx > 0, gx < ngx - 1)
    has_y = (gy > 0, gy < ngy - 1)
    to_x = ({"gx": gx - 1, "gy": gy}, {"gx": gx + 1, "gy": gy})
    to_y = ({"gx": gx, "gy": gy - 1}, {"gx": gx, "gy": gy + 1})
    for s in (0, 1):

        @pl.when(has_y[s])
        def _():
            pl.semaphore_signal(barrier, inc=1, device_id=to_y[s], device_id_type=MESH)

    loads = [
        pltpu.make_async_copy(src, dst, load_sem.at[i])
        for i, (src, dst) in enumerate(
            ((w_hbm, w), (m_hbm, m), (f_hbm, r), (s_hbm, slot), (d_hbm, d))
        )
    ]
    for load in loads:
        load.start()

    n_y = has_y[0].astype(jnp.int32) + has_y[1].astype(jnp.int32)

    def tell(turn):
        for s in (0, 1):

            @pl.when(has_y[s])
            def _():
                pl.semaphore_signal(known.at[turn - 1], inc=1, device_id=to_y[s], device_id_type=MESH)

    def hear(turn):
        pl.semaphore_wait(known.at[turn - 1], n_y)

    edge_x = (0, nx - 1)
    edge_y = (0, ny - 1)

    def remote(src, dst, axis, index, side, target):
        return pltpu.make_async_remote_copy(
            src_ref=src,
            dst_ref=dst.at[1 - side],
            send_sem=sent.at[axis],
            recv_sem=landed.at[axis, index],
            device_id=target,
            device_id_type=MESH,
        )

    def begin(index, src_x, dst_x, src_y, dst_y):
        for s in (0, 1):
            pl.when(has_x[s])(remote(src_x(s), dst_x, 0, index, s, to_x[s]).start)
        for s in (0, 1):
            pl.when(has_y[s])(remote(src_y(s), dst_y, 1, index, s, to_y[s]).start)

    def settle(axis, has, sem, ref, kind):
        target = to_x[0] if axis == 0 else to_y[0]

        def wait(part):
            copy = pltpu.make_async_remote_copy(
                src_ref=part, dst_ref=part, send_sem=sem, recv_sem=sem, device_id=target, device_id_type=MESH
            )
            return getattr(copy, kind)

        pl.when(jnp.logical_and(has[0], has[1]))(wait(ref))
        pl.when(jnp.logical_xor(has[0], has[1]))(wait(ref.at[0]))

    def arrive(index, dst_x, dst_y):
        settle(0, has_x, landed.at[0, index], dst_x, "wait_recv")
        settle(1, has_y, landed.at[1, index], dst_y, "wait_recv")

    loads[0].wait()
    loads[1].wait()
    for x in range(nx):
        phase = m[x]
        cond[x] = jnp.where(phase == 0, 0.2, jnp.where(phase == 1, 1.0, 0.6)).astype(f32) * (0.5 + w[x])
    loads[2].wait()
    for s in (0, 1):
        e = edge_x[s]
        px_first[s, 0] = cond[e]
        px_first[s, 1] = r[e]
        for x in range(nx):
            py_first[s, pl.ds(x, 1), :] = r[x, pl.ds(edge_y[s], 1), :]
            py_first[s, pl.ds(nx + x, 1), :] = cond[x, pl.ds(edge_y[s], 1), :]

        @pl.when(jnp.logical_not(has_x[s]))
        def _():
            hx_first[s] = jnp.zeros((2, ny, nz), f32)
            hx_early[s] = jnp.zeros((2, ny, nz), f32)
            hx_z[s] = jnp.zeros((ny, nz), f32)

        @pl.when(jnp.logical_not(has_y[s]))
        def _():
            hy_first[s] = jnp.zeros((2 * nx, nz), f32)
            hy_early[s] = jnp.zeros((2 * nx, nz), f32)
            hy_z[s] = jnp.zeros((nx, nz), f32)

    pl.semaphore_wait(barrier, ngx - 1 + n_y)
    begin(0, lambda s: px_first.at[s], hx_first, lambda s: py_first.at[s], hy_first)
    if ngy > 1:
        tell(1)
    loads[3].wait()
    loads[4].wait()
    for s in (0, 1):
        e = edge_x[s]
        px_early[s, 0] = slot[e].astype(f32)
        px_early[s, 1] = d[e]
        for x in range(nx):
            py_early[s, pl.ds(x, 1), :] = slot[x, pl.ds(edge_y[s], 1), :].astype(f32)
            py_early[s, pl.ds(nx + x, 1), :] = d[x, pl.ds(edge_y[s], 1), :]
    begin(1, lambda s: px_early.at[s], hx_early, lambda s: py_early.at[s], hy_early)

    lane = lax.broadcasted_iota(jnp.int32, (ny, nz), 1)
    row = lax.broadcasted_iota(jnp.int32, (ny, nz), 0)
    row_high = lax.broadcasted_iota(jnp.int32, (HIGH, nz), 0)
    row_low = lax.broadcasted_iota(jnp.int32, (LOW, nz), 0)

    def spread(ref, y, rows):
        return jnp.broadcast_to(ref[pl.ds(y, 1), :], (rows, nz))

    def low_rows(slots, y):
        low = jnp.bitwise_and(spread(slots, y, LOW), LOW - 1)
        return jnp.where(low == row_low, 1.0, 0.0).astype(bf16)

    def add_row(sums, slots, fields, right, y):
        mask = lax.shift_right_logical(spread(slots, y, HIGH), 4) == row_high
        left = jnp.concatenate([jnp.where(mask, spread(field, y, HIGH), 0.0) for field in fields], axis=0)
        return sums + lax.dot_general(
            left.astype(bf16), right, (((1,), (1,)), ((), ())), preferred_element_type=f32
        )

    def split(high, low, weighted):
        upper = weighted.astype(bf16).astype(f32)
        high[...] = upper
        low[...] = weighted - upper

    for x in range(nx):
        here = cond[x]
        if x > 0:
            lx[x] = harmonic(cond[x - 1], here)
        right = jnp.where(lane == nz - 1, 0.0, harmonic(here, pltpu.roll(here, nz - 1, 1)))
        up = jnp.where(row == ny - 1, 0.0, harmonic(here, pltpu.roll(here, ny - 1, 0)))
        lz[x] = right
        lzleft[x] = pltpu.roll(right, 1, 1)
        ly[x] = up
        lydown[x] = pltpu.roll(up, 1, 0)
    for x in range(nx):
        phase = m[x]
        cap = jnp.where(phase == 0, 1.0, jnp.where(phase == 1, 2.0, 1.5)).astype(f32)
        whole = cap + lz[x] + lzleft[x] + ly[x] + lydown[x]
        if x > 0:
            whole = whole + lx[x]
        if x < nx - 1:
            whole = whole + lx[x + 1]
        diag[x] = whole

    def apply(field, x):
        v = field[x]
        out = diag[x] * v
        if x > 0:
            out = out - lx[x] * field[x - 1]
        if x < nx - 1:
            out = out - lx[x + 1] * field[x + 1]
        out = out - ly[x] * pltpu.roll(v, ny - 1, 0) - lydown[x] * pltpu.roll(v, 1, 0)
        return out - lz[x] * pltpu.roll(v, nz - 1, 1) - lzleft[x] * pltpu.roll(v, 1, 1)

    for x in range(nx):
        z1[x] = apply(r, x)

    def begin_sketch(x, sums):
        split(parts.at[0, x], parts.at[1, x], d[x] * r[x])
        for y in range(ny):
            right = low_rows(slot.at[x], y)
            onehot[x, y] = right
            sums = add_row(sums, slot.at[x], (parts.at[0, x], parts.at[1, x]), right, y)
        return sums

    sums = lax.fori_loop(0, nx, begin_sketch, jnp.zeros((2 * HIGH, LOW), f32))
    mine[...] = jnp.zeros((HIGH, SKETCH), f32)
    mine[:, 0:LOW] = sums[:HIGH] + sums[HIGH:]
    for turn in range(2, ngy):
        hear(turn - 1)
        tell(turn)

    arrive(0, hx_first, hy_first)
    for s in (0, 1):
        e = edge_x[s]
        link = harmonic(hx_first[s, 0], cond[e])
        lx[nx * s] = link
        z1[e] = z1[e] + link * (r[e] - hx_first[s, 1])
    for s in (0, 1):
        for x in range(nx):
            here, there = pl.ds(x, 1), pl.ds(nx + x, 1)
            link = harmonic(hy_first[s, there, :], py_first[s, there, :])
            lyb[s, here, :] = link
            flux = link * (py_first[s, here, :] - hy_first[s, here, :])
            after = z1[x, pl.ds(edge_y[s], 1), :] + flux
            z1[x, pl.ds(edge_y[s], 1), :] = after
            py_z[s, here, :] = after
    begin(2, lambda s: z1.at[edge_x[s]], hx_z, lambda s: py_z.at[s], hy_z)
    for x in range(nx):
        out = apply(z1, x)
        for s in (0, 1):
            if x == edge_x[s]:
                out = out + lx[nx * s] * z1[x]
        z2[x] = out
        for s in (0, 1):
            at = (x, pl.ds(edge_y[s], 1), slice(None))
            z2[at] = z2[at] + lyb[s, pl.ds(x, 1), :] * py_z[s, pl.ds(x, 1), :]
    sums = jnp.zeros((4 * HIGH, LOW), f32)
    for x in range(nx):
        split(parts.at[0, x], parts.at[1, x], d[x] * z1[x])
        split(parts.at[2, x], parts.at[3, x], d[x] * z2[x])
        for y in range(ny):
            sums = add_row(sums, slot.at[x], [parts.at[k, x] for k in range(4)], onehot[x, y], y)
    arrive(1, hx_early, hy_early)
    edge_sums = jnp.zeros((2 * HIGH, LOW), f32)
    for s in (0, 1):
        split(wedge.at[0, s], wedge.at[1, s], -lx[nx * s] * z1[edge_x[s]] * hx_early[s, 1])
        sedge[s] = hx_early[s, 0].astype(jnp.int32)
        for x in range(nx):
            at = pl.ds(s * nx + x, 1)
            edge = -lyb[s, pl.ds(x, 1), :] * py_z[s, pl.ds(x, 1), :] * hy_early[s, pl.ds(nx + x, 1), :]
            upper = edge.astype(bf16).astype(f32)
            wedge[0, 2, at, :] = upper
            wedge[1, 2, at, :] = edge - upper
            sedge[2, at, :] = hy_early[s, pl.ds(x, 1), :].astype(jnp.int32)
    for t in range(3):
        for y in range(ny if t < 2 else 2 * nx):
            edge_sums = add_row(edge_sums, sedge.at[t], (wedge.at[0, t], wedge.at[1, t]), low_rows(sedge.at[t], y), y)
    mine[:, LOW : 2 * LOW] = sums[:HIGH] + sums[HIGH : 2 * HIGH]
    mine[:, 2 * LOW : 3 * LOW] = (
        sums[2 * HIGH : 3 * HIGH] + sums[3 * HIGH :] + edge_sums[:HIGH] + edge_sums[HIGH:]
    )

    def share(step, carry):
        pltpu.make_async_remote_copy(
            src_ref=mine,
            dst_ref=gathered.at[me],
            send_sem=share_sem.at[0],
            recv_sem=share_sem.at[1],
            device_id=peer(step),
            device_id_type=MESH,
        ).start()
        return carry

    if ngy > 1:
        hear(ngy - 1)
    lax.fori_loop(1, count, share, 0)
    gathered[me] = mine[...]
    arrive(2, hx_z, hy_z)
    for s in (0, 1):
        z2[edge_x[s]] = z2[edge_x[s]] - lx[nx * s] * hx_z[s]
        for x in range(nx):
            at = (x, pl.ds(edge_y[s], 1), slice(None))
            z2[at] = z2[at] - lyb[s, pl.ds(x, 1), :] * hy_z[s, pl.ds(x, 1), :]
    others = gathered.at[pl.ds(0, count - 1)]
    shared = pltpu.make_async_remote_copy(
        src_ref=others,
        dst_ref=others,
        send_sem=share_sem.at[0],
        recv_sem=share_sem.at[1],
        device_id=peer(1),
        device_id_type=MESH,
    )
    shared.wait_recv()
    summed = jnp.sum(gathered[...], axis=0)
    c0, c1 = coefficients(*(summed[:, k * LOW : (k + 1) * LOW] for k in range(3)))
    for x in range(nx):
        answer[x] = c0 * r[x] + c1 * z1[x]
        rest[x] = r[x] - c0 * z1[x] - c1 * z2[x]
    shared.wait_send()
    settle(0, has_x, sent.at[0], bulk_x, "wait_send")
    settle(1, has_y, sent.at[1], bulk_y, "wait_send")


def put_out(answer, rest, answer_out, rest_out, sem):
    one = pltpu.make_async_copy(answer, answer_out, sem.at[0])
    two = pltpu.make_async_copy(rest, rest_out, sem.at[1])
    one.start()
    two.start()
    one.wait()
    two.wait()


def body(ngx, ngy, f, w, m, s, d):
    nx, ny, nz = f.shape
    count = ngx * ngy
    vm = lambda shape, dtype=f32: pltpu.VMEM(shape, dtype)
    block = (nx, ny, nz)
    assert 2 * nx <= ny
    answer, rest = pl.pallas_call(
        functools.partial(kernel, ngx, ngy, nx, ny, nz),
        out_shape=(vm(block), vm(block)),
        in_specs=[pl.BlockSpec(memory_space=pl.ANY)] * 5,
        out_specs=[pl.BlockSpec(memory_space=pltpu.VMEM)] * 2,
        scratch_shapes=[
            vm(block), vm(block),
            vm(block), vm(block), vm(block, jnp.int32), vm(block, jnp.int32), vm(block),
            vm(block), vm(block),
            vm((nx + 1, ny, nz)), vm(block), vm(block), vm(block), vm(block), vm((2, nx, nz)),
            vm((nx, ny, LOW, nz), bf16), vm((4, nx, ny, nz)), vm((2, 3, ny, nz)), vm((3, ny, nz), jnp.int32),
            vm((2, 2, ny, nz)), vm((2, 2, ny, nz)), vm((2, ny, nz)), vm((2, 2 * nx, nz)), vm((2, 2 * nx, nz)), vm((2, nx, nz)),
            vm((2, 2, ny, nz)), vm((2, 2, ny, nz)), vm((2, 2 * nx, nz)), vm((2, 2 * nx, nz)), vm((2, nx, nz)),
            vm((2, 5, ny, nz)), vm((2, 5, nx, nz)),
            vm((HIGH, SKETCH)), vm((count, HIGH, SKETCH)),
            pltpu.SemaphoreType.DMA((5,)),
            pltpu.SemaphoreType.DMA((2,)),
            pltpu.SemaphoreType.DMA((2, 3)),
            pltpu.SemaphoreType.DMA((2,)),
            pltpu.SemaphoreType.REGULAR((max(ngy - 1, 1),)),
        ],
        compiler_params=pltpu.CompilerParams(collective_id=0, has_side_effects=True),
        name="sketched_gmres",
    )(f, w, m, s, d)
    return pl.pallas_call(
        put_out,
        out_shape=(jax.ShapeDtypeStruct(block, f32), jax.ShapeDtypeStruct(block, f32)),
        in_specs=[pl.BlockSpec(memory_space=pltpu.VMEM)] * 2,
        out_specs=[pl.BlockSpec(memory_space=pl.ANY)] * 2,
        scratch_shapes=[pltpu.SemaphoreType.DMA((2,))],
        name="put_out",
    )(pltpu.with_memory_space_constraint(answer, pltpu.VMEM), pltpu.with_memory_space_constraint(rest, pltpu.VMEM))


def solution(mesh):
    spec = P(("parts", "gx"), "gy", None)
    return jax.shard_map(
        functools.partial(body, mesh.shape["gx"], mesh.shape["gy"]),
        mesh=mesh,
        in_specs=(spec,) * 5,
        out_specs=(spec, spec),
        check_vma=False,
    )
```

time: 16.6 us -> 15.9 us (0.958)
  Pallas kernels: 15.8 us -> 15.1 us
    pallas_call x1, Pallas kernels: 15.1 us -> 14.4 us  [body(): pl.pallas_call(functools.partial(kernel, ngx, ngy, nx, ny, nz), out_shape...]
where the time goes in v2:
time: 15.9 us; the launch traced here: 15.7 us
  Pallas kernels  15.1 us (95%)
  between operations  0.64 us (4%)
    pallas_call x1, Pallas kernels, body(): pl.pallas_call(functools.partial(kernel, ngx, ngy, nx, ny, nz), out_shape...  14.4 us
    pallas_call x1, Pallas kernels, body(): pl.pallas_call(put_out, out_shape=(jax.ShapeDtypeStruct(block, f32), jax....  0.72 us

profile of v2, /device:TPU:0, one launch (start us, length us, event | category | flops | bytes accessed | tf_op | source)
XLA Modules:
  0.0 15.7 jit_solution(8444160155017367144)
XLA Ops:
  0.6 14.4 %sketched_gmres.1 = (f32[4,8,1024]{2,1,0:T(8,128)S(1)}, f32[4,8,1024]{2,1,0:T(8,128)S(1)}) custom-call(f32[4,8,1024]{2,1,0:T(8,128)} %f_hbm.1, f32[4,8,1024]{2,1,0:T(8,128)} %w_hbm.1, s32[4,8,1024]{2,1,0:T(8,128)} %m_hbm.1, s32[4,8,1024]{2,1,0:T(8,128)} %s_hbm.1, f32[4,8,1024]{2,1,0:T(8,128)} %d_hbm.1), custom_call_target="tpu_custom_call" | custom-call | tf_op jit(solution)/shard_map/sketched_gmres/pallas_call | solution.py:355
  15.0 0.7 %put_out.1 = (f32[4,8,1024]{2,1,0:T(8,128)}, f32[4,8,1024]{2,1,0:T(8,128)}) custom-call(f32[4,8,1024]{2,1,0:T(8,128)S(1)} %get-tuple-element.4.answer, f32[4,8,1024]{2,1,0:T(8,128)S(1)} %get-tuple-element.5.rest), custom_call_target="tpu_custom_call" | custom-call | tf_op jit(solution)/shard_map/put_out/pallas_call | solution.py:379

commit v3 on v2

--- a/solution.py
+++ b/solution.py
@@ -32,10 +32,13 @@
     w1 = s2 - h00 * s1
     n0sq = total(t0 * t0) * inv_beta2 + epsilon
     cross = total(s0 * w1) * inv_beta2
+    along = total(t0 * w1) * inv_beta2
+    whole = total(w1 * w1) * inv_beta2
     inv_n0sq = 1.0 / n0sq
-    h11 = total(t0 * w1) * inv_beta2 * inv_n0sq
-    t1 = w1 - cross * s0 - h11 * t0
-    n1sq = total(t1 * t1) * inv_beta2 * inv_n0sq + epsilon
+    h11 = along * inv_n0sq
+    shift = epsilon * inv_beta2
+    left = whole - cross * cross * (1.0 + shift) - h11 * h11 * (n0sq + epsilon) + 2.0 * cross * h11 * h00 * shift
+    n1sq = jnp.maximum(left, 0.0) * inv_n0sq + epsilon
     minor = h00 * h11 - cross
     inv_det = 1.0 / (minor * minor + n1sq * (h00 * h00 + n0sq))
     return (minor * (h11 + h00) + h00 * n1sq) * inv_det, -minor * inv_det
@@ -45,7 +48,7 @@
     ngx, ngy, nx, ny, nz,
     f_hbm, w_hbm, m_hbm, s_hbm, d_hbm,
     answer, rest,
-    z1, z2, r, w, m, slot, d, cond, diag, lx, ly, lydown, lz, lzleft, lyb, onehot, parts, wedge, sedge,
+    z1, z2, r, w, m, slot, d, cond, diag, lx, ly, lydown, lz, lzleft, lyb, onehot, onehot_edge, parts, wedge, sedge,
     hx_first, hx_early, hx_z, hy_first, hy_early, hy_z,
     px_first, px_early, py_first, py_early, py_z,
     bulk_x, bulk_y, mine, gathered, load_sem, sent, landed, share_sem, known,
@@ -87,15 +90,14 @@
 
     n_y = has_y[0].astype(jnp.int32) + has_y[1].astype(jnp.int32)
 
-    def tell(turn):
-        for s in (0, 1):
-
-            @pl.when(has_y[s])
-            def _():
-                pl.semaphore_signal(known.at[turn - 1], inc=1, device_id=to_y[s], device_id_type=MESH)
-
-    def hear(turn):
-        pl.semaphore_wait(known.at[turn - 1], n_y)
+    def tell(side):
+        pl.semaphore_signal(known.at[side], inc=1, device_id=to_y[side], device_id_type=MESH)
+
+    def pass_on(side):
+        pl.semaphore_wait(known.at[side], 1)
+        tell(side)
+
+    middle = jnp.logical_and(has_y[0], has_y[1])
 
     edge_x = (0, nx - 1)
     edge_y = (0, ny - 1)
@@ -161,7 +163,9 @@
     pl.semaphore_wait(barrier, ngx - 1 + n_y)
     begin(0, lambda s: px_first.at[s], hx_first, lambda s: py_first.at[s], hy_first)
     if ngy > 1:
-        tell(1)
+        pl.when(gy == 0)(functools.partial(tell, 1))
+        pl.when(gy == ngy - 1)(functools.partial(tell, 0))
+        pl.when(middle)(functools.partial(pass_on, 1))
     loads[3].wait()
     loads[4].wait()
     for s in (0, 1):
@@ -179,7 +183,8 @@
     row_low = lax.broadcasted_iota(jnp.int32, (LOW, nz), 0)
 
     def spread(ref, y, rows):
-        return jnp.broadcast_to(ref[pl.ds(y, 1), :], (rows, nz))
+        part = ref[pl.ds(y, 8, stride=0), :]
+        return part if rows == 8 else jnp.concatenate([part] * (rows // 8), axis=0)
 
     def low_rows(slots, y):
         low = jnp.bitwise_and(spread(slots, y, LOW), LOW - 1)
@@ -241,9 +246,8 @@
     sums = lax.fori_loop(0, nx, begin_sketch, jnp.zeros((2 * HIGH, LOW), f32))
     mine[...] = jnp.zeros((HIGH, SKETCH), f32)
     mine[:, 0:LOW] = sums[:HIGH] + sums[HIGH:]
-    for turn in range(2, ngy):
-        hear(turn - 1)
-        tell(turn)
+    if ngy > 1:
+        pl.when(middle)(functools.partial(pass_on, 0))
 
     arrive(0, hx_first, hy_first)
     for s in (0, 1):
@@ -261,6 +265,7 @@
             z1[x, pl.ds(edge_y[s], 1), :] = after
             py_z[s, here, :] = after
     begin(2, lambda s: z1.at[edge_x[s]], hx_z, lambda s: py_z.at[s], hy_z)
+    chains = [jnp.zeros((4 * HIGH, LOW), f32) for _ in range(2)]
     for x in range(nx):
         out = apply(z1, x)
         for s in (0, 1):
@@ -270,14 +275,12 @@
         for s in (0, 1):
             at = (x, pl.ds(edge_y[s], 1), slice(None))
             z2[at] = z2[at] + lyb[s, pl.ds(x, 1), :] * py_z[s, pl.ds(x, 1), :]
-    sums = jnp.zeros((4 * HIGH, LOW), f32)
-    for x in range(nx):
         split(parts.at[0, x], parts.at[1, x], d[x] * z1[x])
         split(parts.at[2, x], parts.at[3, x], d[x] * z2[x])
         for y in range(ny):
-            sums = add_row(sums, slot.at[x], [parts.at[k, x] for k in range(4)], onehot[x, y], y)
+            chains[y % 2] = add_row(chains[y % 2], slot.at[x], [parts.at[k, x] for k in range(4)], onehot[x, y], y)
     arrive(1, hx_early, hy_early)
-    edge_sums = jnp.zeros((2 * HIGH, LOW), f32)
+    edge_chains = [jnp.zeros((2 * HIGH, LOW), f32) for _ in range(2)]
     for s in (0, 1):
         split(wedge.at[0, s], wedge.at[1, s], -lx[nx * s] * z1[edge_x[s]] * hx_early[s, 1])
         sedge[s] = hx_early[s, 0].astype(jnp.int32)
@@ -290,11 +293,20 @@
             sedge[2, at, :] = hy_early[s, pl.ds(x, 1), :].astype(jnp.int32)
     for t in range(3):
         for y in range(ny if t < 2 else 2 * nx):
-            edge_sums = add_row(edge_sums, sedge.at[t], (wedge.at[0, t], wedge.at[1, t]), low_rows(sedge.at[t], y), y)
-    mine[:, LOW : 2 * LOW] = sums[:HIGH] + sums[HIGH : 2 * HIGH]
-    mine[:, 2 * LOW : 3 * LOW] = (
-        sums[2 * HIGH : 3 * HIGH] + sums[3 * HIGH :] + edge_sums[:HIGH] + edge_sums[HIGH:]
-    )
+            onehot_edge[t, y] = low_rows(sedge.at[t], y)
+    for t in range(3):
+        for y in range(ny if t < 2 else 2 * nx):
+            edge_chains[y % 2] = add_row(edge_chains[y % 2], sedge.at[t], (wedge.at[0, t], wedge.at[1, t]), onehot_edge[t, y], y)
+    def placed(block, k):
+        wide = jnp.concatenate([block, jnp.zeros((HIGH, SKETCH - LOW), f32)], axis=1)
+        return pltpu.roll(wide, k * LOW, 1)
+
+    out = mine[...]
+    for sums, edge_sums in zip(chains, edge_chains):
+        out = out + placed(sums[:HIGH] + sums[HIGH : 2 * HIGH], 1)
+        out = out + placed(sums[2 * HIGH : 3 * HIGH] + sums[3 * HIGH :], 2)
+        out = out + placed(edge_sums[:HIGH] + edge_sums[HIGH:], 2)
+    mine[...] = out
 
     def share(step, carry):
         pltpu.make_async_remote_copy(
@@ -307,8 +319,12 @@
         ).start()
         return carry
 
-    if ngy > 1:
-        hear(ngy - 1)
+    for s in (0, 1):
+
+        @pl.when(jnp.logical_and(has_y[1 - s], jnp.logical_not(has_y[s])))
+        def _():
+            pl.semaphore_wait(known.at[s], 1)
+
     lax.fori_loop(1, count, share, 0)
     gathered[me] = mine[...]
     arrive(2, hx_z, hy_z)
@@ -328,7 +344,10 @@
     )
     shared.wait_recv()
     summed = jnp.sum(gathered[...], axis=0)
-    c0, c1 = coefficients(*(summed[:, k * LOW : (k + 1) * LOW] for k in range(3)))
+    first_lanes = lax.broadcasted_iota(jnp.int32, (HIGH, SKETCH), 1) < LOW
+    c0, c1 = coefficients(
+        *(jnp.where(first_lanes, pltpu.roll(summed, SKETCH - k * LOW, 1) if k else summed, 0.0) for k in range(3))
+    )
     for x in range(nx):
         answer[x] = c0 * r[x] + c1 * z1[x]
         rest[x] = r[x] - c0 * z1[x] - c1 * z2[x]
@@ -362,7 +381,7 @@
             vm(block), vm(block), vm(block, jnp.int32), vm(block, jnp.int32), vm(block),
             vm(block), vm(block),
             vm((nx + 1, ny, nz)), vm(block), vm(block), vm(block), vm(block), vm((2, nx, nz)),
-            vm((nx, ny, LOW, nz), bf16), vm((4, nx, ny, nz)), vm((2, 3, ny, nz)), vm((3, ny, nz), jnp.int32),
+            vm((nx, ny, LOW, nz), bf16), vm((3, ny, LOW, nz), bf16), vm((4, nx, ny, nz)), vm((2, 3, ny, nz)), vm((3, ny, nz), jnp.int32),
             vm((2, 2, ny, nz)), vm((2, 2, ny, nz)), vm((2, ny, nz)), vm((2, 2 * nx, nz)), vm((2, 2 * nx, nz)), vm((2, nx, nz)),
             vm((2, 2, ny, nz)), vm((2, 2, ny, nz)), vm((2, 2 * nx, nz)), vm((2, 2 * nx, nz)), vm((2, nx, nz)),
             vm((2, 5, ny, nz)), vm((2, 5, nx, nz)),
@@ -371,7 +390,7 @@
             pltpu.SemaphoreType.DMA((2,)),
             pltpu.SemaphoreType.DMA((2, 3)),
             pltpu.SemaphoreType.DMA((2,)),
-            pltpu.SemaphoreType.REGULAR((max(ngy - 1, 1),)),
+            pltpu.SemaphoreType.REGULAR((2,)),
         ],
         compiler_params=pltpu.CompilerParams(collective_id=0, has_side_effects=True),
         name="sketched_gmres",

time: 15.9 us -> 15.2 us (0.956)
  Pallas kernels: 15.1 us -> 14.4 us
    pallas_call x1, Pallas kernels: 14.4 us -> 13.7 us  [body(): pl.pallas_call(functools.partial(kernel, ngx, ngy, nx, ny, nz), out_shape...]
where the time goes in v3:
time: 15.2 us; the launch traced here: 15 us
  Pallas kernels  14.4 us (95%)
  between operations  0.64 us (4%)
    pallas_call x1, Pallas kernels, body(): pl.pallas_call(functools.partial(kernel, ngx, ngy, nx, ny, nz), out_shape...  13.7 us
    pallas_call x1, Pallas kernels, body(): pl.pallas_call(put_out, out_shape=(jax.ShapeDtypeStruct(block, f32), jax....  0.72 us

profile of v3, /device:TPU:0, one launch (start us, length us, event | category | flops | bytes accessed | tf_op | source)
XLA Modules:
  0.0 15.0 jit_solution(1066785160248150898)
XLA Ops:
  0.6 13.7 %sketched_gmres.1 = (f32[4,8,1024]{2,1,0:T(8,128)S(1)}, f32[4,8,1024]{2,1,0:T(8,128)S(1)}) custom-call(f32[4,8,1024]{2,1,0:T(8,128)} %f_hbm.1, f32[4,8,1024]{2,1,0:T(8,128)} %w_hbm.1, s32[4,8,1024]{2,1,0:T(8,128)} %m_hbm.1, s32[4,8,1024]{2,1,0:T(8,128)} %s_hbm.1, f32[4,8,1024]{2,1,0:T(8,128)} %d_hbm.1), custom_call_target="tpu_custom_call" | custom-call | tf_op jit(solution)/shard_map/sketched_gmres/pallas_call | solution.py:374
  14.3 0.7 %put_out.1 = (f32[4,8,1024]{2,1,0:T(8,128)}, f32[4,8,1024]{2,1,0:T(8,128)}) custom-call(f32[4,8,1024]{2,1,0:T(8,128)S(1)} %get-tuple-element.4.answer, f32[4,8,1024]{2,1,0:T(8,128)S(1)} %get-tuple-element.5.rest), custom_call_target="tpu_custom_call" | custom-call | tf_op jit(solution)/shard_map/put_out/pallas_call | solution.py:398

commit v4 on v3

--- a/solution.py
+++ b/solution.py
@@ -10,6 +10,7 @@
 SKETCH = 128
 LOW = 16
 HIGH = SKETCH // LOW
+WIDE = 32
 MESH = pl.DeviceIdType.MESH
 epsilon = 1e-06
 highest = lax.Precision.HIGHEST
@@ -48,10 +49,10 @@
     ngx, ngy, nx, ny, nz,
     f_hbm, w_hbm, m_hbm, s_hbm, d_hbm,
     answer, rest,
-    z1, z2, r, w, m, slot, d, cond, diag, lx, ly, lydown, lz, lzleft, lyb, onehot, onehot_edge, parts, wedge, sedge,
+    z1, z2, r, w, m, slot, d, cond, diag, lx, ly, lydown, lz, lzleft, lyb, onehot, highs, onehot_edge, parts, wedge, sedge,
     hx_first, hx_early, hx_z, hy_first, hy_early, hy_z,
     px_first, px_early, py_first, py_early, py_z,
-    bulk_x, bulk_y, mine, gathered, load_sem, sent, landed, share_sem, known,
+    bulk_x, bulk_y, mine, gathered, load_sem, sent, landed, beside, share_sem, known,
 ):
     gx = lax.axis_index("gx")
     gy = lax.axis_index("gy")
@@ -59,15 +60,13 @@
     me = gx * ngy + gy
 
 
+    mine_at = gy * ngx + gx
+
     def peer(step):
-        other = lax.rem(me + step, count)
-        return {"gx": lax.div(other, ngy), "gy": lax.rem(other, ngy)}
+        other = step + (step >= mine_at).astype(jnp.int32)
+        return {"gx": lax.rem(other, ngx), "gy": lax.div(other, ngx)}
 
     barrier = pltpu.get_barrier_semaphore()
-
-    for step in range(1, ngx):
-        other = {"gx": lax.rem(gx + step, ngx), "gy": gy}
-        pl.semaphore_signal(barrier, inc=1, device_id=other, device_id_type=MESH)
 
     has_x = (gx > 0, gx < ngx - 1)
     has_y = (gy > 0, gy < ngy - 1)
@@ -79,11 +78,13 @@
         def _():
             pl.semaphore_signal(barrier, inc=1, device_id=to_y[s], device_id_type=MESH)
 
+    for step in range(1, ngx):
+        other = {"gx": lax.rem(gx + step, ngx), "gy": gy}
+        pl.semaphore_signal(barrier, inc=1, device_id=other, device_id_type=MESH)
+
     loads = [
         pltpu.make_async_copy(src, dst, load_sem.at[i])
-        for i, (src, dst) in enumerate(
-            ((w_hbm, w), (m_hbm, m), (f_hbm, r), (s_hbm, slot), (d_hbm, d))
-        )
+        for i, src, dst in ((0, w_hbm, w), (0, m_hbm, m), (1, f_hbm, r), (2, s_hbm, slot), (2, d_hbm, d))
     ]
     for load in loads:
         load.start()
@@ -101,22 +102,27 @@
 
     edge_x = (0, nx - 1)
     edge_y = (0, ny - 1)
+
+    def arrival(axis, index, side):
+        if axis == 0 and index == 1:
+            return beside.at[side]
+        return landed.at[(0, None, 1)[index] if axis == 0 else 2 + index]
 
     def remote(src, dst, axis, index, side, target):
         return pltpu.make_async_remote_copy(
             src_ref=src,
             dst_ref=dst.at[1 - side],
             send_sem=sent.at[axis],
-            recv_sem=landed.at[axis, index],
+            recv_sem=arrival(axis, index, 1 - side),
             device_id=target,
             device_id_type=MESH,
         )
 
     def begin(index, src_x, dst_x, src_y, dst_y):
         for s in (0, 1):
+            pl.when(has_y[s])(remote(src_y(s), dst_y, 1, index, s, to_y[s]).start)
+        for s in (0, 1):
             pl.when(has_x[s])(remote(src_x(s), dst_x, 0, index, s, to_x[s]).start)
-        for s in (0, 1):
-            pl.when(has_y[s])(remote(src_y(s), dst_y, 1, index, s, to_y[s]).start)
 
     def settle(axis, has, sem, ref, kind):
         target = to_x[0] if axis == 0 else to_y[0]
@@ -131,11 +137,29 @@
         pl.when(jnp.logical_xor(has[0], has[1]))(wait(ref.at[0]))
 
     def arrive(index, dst_x, dst_y):
-        settle(0, has_x, landed.at[0, index], dst_x, "wait_recv")
-        settle(1, has_y, landed.at[1, index], dst_y, "wait_recv")
-
-    loads[0].wait()
-    loads[1].wait()
+        settle(0, has_x, arrival(0, index, 0), dst_x, "wait_recv")
+        settle(1, has_y, arrival(1, index, 0), dst_y, "wait_recv")
+
+    far = jnp.bitwise_and(gx, 1)
+    near = 1 - far
+
+    def arrive_beside(side):
+        copy = pltpu.make_async_remote_copy(
+            src_ref=hx_early.at[side],
+            dst_ref=hx_early.at[side],
+            send_sem=sent.at[0],
+            recv_sem=beside.at[side],
+            device_id=to_x[0],
+            device_id_type=MESH,
+        )
+        pl.when(jnp.logical_or(jnp.logical_and(side == 0, has_x[0]), jnp.logical_and(side == 1, has_x[1])))(copy.wait_recv)
+
+    two_blocks = parts.at[pl.ds(0, nx // 2)]
+
+    def both_loaded(i):
+        pltpu.make_async_copy(two_blocks, two_blocks, load_sem.at[i]).wait()
+
+    both_loaded(0)
     for x in range(nx):
         phase = m[x]
         cond[x] = jnp.where(phase == 0, 0.2, jnp.where(phase == 1, 1.0, 0.6)).astype(f32) * (0.5 + w[x])
@@ -165,9 +189,7 @@
     if ngy > 1:
         pl.when(gy == 0)(functools.partial(tell, 1))
         pl.when(gy == ngy - 1)(functools.partial(tell, 0))
-        pl.when(middle)(functools.partial(pass_on, 1))
-    loads[3].wait()
-    loads[4].wait()
+    both_loaded(2)
     for s in (0, 1):
         e = edge_x[s]
         px_early[s, 0] = slot[e].astype(f32)
@@ -179,8 +201,11 @@
 
     lane = lax.broadcasted_iota(jnp.int32, (ny, nz), 1)
     row = lax.broadcasted_iota(jnp.int32, (ny, nz), 0)
-    row_high = lax.broadcasted_iota(jnp.int32, (HIGH, nz), 0)
+    place = lax.broadcasted_iota(jnp.int32, (HIGH, nz), 0)
+    row_half = lax.shift_right_logical(place, 2)
+    row_high = 2 * row_half + 4 * jnp.bitwise_and(lax.shift_right_logical(place, 1), 1) + jnp.bitwise_and(place, 1)
     row_low = lax.broadcasted_iota(jnp.int32, (LOW, nz), 0)
+    row_wide = lax.broadcasted_iota(jnp.int32, (WIDE, nz), 0)
 
     def spread(ref, y, rows):
         part = ref[pl.ds(y, 8, stride=0), :]
@@ -235,20 +260,62 @@
     for x in range(nx):
         z1[x] = apply(r, x)
 
+    def split_into(x, k, weighted):
+        upper = weighted.astype(bf16).astype(f32)
+        lower = weighted - upper
+        for t in range(nz // SKETCH):
+            at = slice(t * SKETCH, (t + 1) * SKETCH)
+            parts[x, t, pl.ds(k, ny, stride=4), :] = upper[:, at]
+            parts[x, t, pl.ds(k + 1, ny, stride=4), :] = lower[:, at]
+
+    def masked(x, y):
+        pair = jnp.concatenate([parts[x, t, pl.ds(y // 2 * 8, 8), :] for t in range(nz // SKETCH)], axis=1)
+        swapped = pltpu.roll(pair, 4, 0)
+        both = jnp.where(place < 4, pair, swapped) if y % 2 == 0 else jnp.where(place < 4, swapped, pair)
+        return jnp.concatenate([both, both], axis=0).astype(bf16) * highs[x, y]
+
+    def matmul(left, right):
+        return lax.dot_general(left, right, (((1,), (1,)), ((), ())), preferred_element_type=f32)
+
     def begin_sketch(x, sums):
-        split(parts.at[0, x], parts.at[1, x], d[x] * r[x])
+        split_into(x, 0, d[x] * r[x])
+        split_into(x, 2, jnp.zeros((ny, nz), f32))
         for y in range(ny):
-            right = low_rows(slot.at[x], y)
+            low = jnp.bitwise_and(spread(slot.at[x], y, WIDE), WIDE - 1)
+            right = jnp.where(low == row_wide, 1.0, 0.0).astype(bf16)
             onehot[x, y] = right
-            sums = add_row(sums, slot.at[x], (parts.at[0, x], parts.at[1, x]), right, y)
+            high = lax.shift_right_logical(spread(slot.at[x], y, HIGH), 5)
+            mask = [jnp.where(high == row_half + 2 * k, 1.0, 0.0) for k in (0, 1)]
+            highs[x, y] = jnp.concatenate(mask, axis=0).astype(bf16)
+            sums = sums + matmul(masked(x, y), right)
         return sums
 
-    sums = lax.fori_loop(0, nx, begin_sketch, jnp.zeros((2 * HIGH, LOW), f32))
-    mine[...] = jnp.zeros((HIGH, SKETCH), f32)
-    mine[:, 0:LOW] = sums[:HIGH] + sums[HIGH:]
+    column = lax.broadcasted_iota(jnp.int32, (HIGH, SKETCH), 1)
+    place_row = lax.broadcasted_iota(jnp.int32, (HIGH, SKETCH), 0)
+
+    def padded(block):
+        return jnp.concatenate([block, jnp.zeros((HIGH, SKETCH - block.shape[1]), f32)], axis=1)
+
+    def turned(wide, rows, columns):
+        wide = pltpu.roll(wide, rows % HIGH, 0) if rows % HIGH else wide
+        return pltpu.roll(wide, columns % SKETCH, 1) if columns % SKETCH else wide
+
+    def folded(sums, base, k):
+        low, high = padded(sums[:HIGH]), padded(sums[HIGH:])
+        low = turned(low + turned(low, -1, 0), -base, 0)
+        high = turned(high + turned(high, -1, 0), -base, 0)
+        quarter = jnp.bitwise_and(place_row, 3)
+        even = turned(jnp.where(quarter == 0, low, turned(high, 2, 0)), 0, k * LOW)
+        odd = turned(jnp.where(quarter == 1, turned(low, 1, 0), turned(high, 3, 0)), 0, (k - 1) * LOW)
+        out = jnp.where(jnp.bitwise_and(place_row, 1) == 0, even, odd)
+        return jnp.where(lax.div(column, LOW) == k, out, 0.0)
+
+    mine[...] = folded(lax.fori_loop(0, nx, begin_sketch, jnp.zeros((2 * HIGH, WIDE), f32)), 0, 3)
     if ngy > 1:
+        pl.when(middle)(functools.partial(pass_on, 1))
         pl.when(middle)(functools.partial(pass_on, 0))
 
+    arrive_beside(near)
     arrive(0, hx_first, hy_first)
     for s in (0, 1):
         e = edge_x[s]
@@ -265,7 +332,7 @@
             z1[x, pl.ds(edge_y[s], 1), :] = after
             py_z[s, here, :] = after
     begin(2, lambda s: z1.at[edge_x[s]], hx_z, lambda s: py_z.at[s], hy_z)
-    chains = [jnp.zeros((4 * HIGH, LOW), f32) for _ in range(2)]
+    chains = [jnp.zeros((2 * HIGH, WIDE), f32) for _ in range(2)]
     for x in range(nx):
         out = apply(z1, x)
         for s in (0, 1):
@@ -275,37 +342,42 @@
         for s in (0, 1):
             at = (x, pl.ds(edge_y[s], 1), slice(None))
             z2[at] = z2[at] + lyb[s, pl.ds(x, 1), :] * py_z[s, pl.ds(x, 1), :]
-        split(parts.at[0, x], parts.at[1, x], d[x] * z1[x])
-        split(parts.at[2, x], parts.at[3, x], d[x] * z2[x])
+        split_into(x, 0, d[x] * z1[x])
+        split_into(x, 2, d[x] * z2[x])
         for y in range(ny):
-            chains[y % 2] = add_row(chains[y % 2], slot.at[x], [parts.at[k, x] for k in range(4)], onehot[x, y], y)
-    arrive(1, hx_early, hy_early)
+            chains[y % 2] = chains[y % 2] + matmul(masked(x, y), onehot[x, y])
     edge_chains = [jnp.zeros((2 * HIGH, LOW), f32) for _ in range(2)]
-    for s in (0, 1):
-        split(wedge.at[0, s], wedge.at[1, s], -lx[nx * s] * z1[edge_x[s]] * hx_early[s, 1])
-        sedge[s] = hx_early[s, 0].astype(jnp.int32)
+
+    def sketch_edge(t, rows):
+        for y in range(rows):
+            onehot_edge[t, y] = low_rows(sedge.at[t], y)
+        for y in range(rows):
+            edge_chains[y % 2] = add_row(
+                edge_chains[y % 2], sedge.at[t], (wedge.at[0, t], wedge.at[1, t]), onehot_edge[t, y], y
+            )
+
+    def face_edge(t, side):
+        split(wedge.at[0, t], wedge.at[1, t], -lx[nx * side] * z1[(nx - 1) * side] * hx_early[side, 1])
+        sedge[t] = hx_early[side, 0].astype(jnp.int32)
+        sketch_edge(t, ny)
+
+    face_edge(0, near)
+    settle(1, has_y, arrival(1, 1, 0), hy_early, "wait_recv")
+    for s in (0, 1):
         for x in range(nx):
             at = pl.ds(s * nx + x, 1)
             edge = -lyb[s, pl.ds(x, 1), :] * py_z[s, pl.ds(x, 1), :] * hy_early[s, pl.ds(nx + x, 1), :]
             upper = edge.astype(bf16).astype(f32)
-            wedge[0, 2, at, :] = upper
-            wedge[1, 2, at, :] = edge - upper
-            sedge[2, at, :] = hy_early[s, pl.ds(x, 1), :].astype(jnp.int32)
-    for t in range(3):
-        for y in range(ny if t < 2 else 2 * nx):
-            onehot_edge[t, y] = low_rows(sedge.at[t], y)
-    for t in range(3):
-        for y in range(ny if t < 2 else 2 * nx):
-            edge_chains[y % 2] = add_row(edge_chains[y % 2], sedge.at[t], (wedge.at[0, t], wedge.at[1, t]), onehot_edge[t, y], y)
-    def placed(block, k):
-        wide = jnp.concatenate([block, jnp.zeros((HIGH, SKETCH - LOW), f32)], axis=1)
-        return pltpu.roll(wide, k * LOW, 1)
-
+            wedge[0, 1, at, :] = upper
+            wedge[1, 1, at, :] = edge - upper
+            sedge[1, at, :] = hy_early[s, pl.ds(x, 1), :].astype(jnp.int32)
+    sketch_edge(1, 2 * nx)
+    arrive_beside(far)
+    face_edge(2, far)
     out = mine[...]
     for sums, edge_sums in zip(chains, edge_chains):
-        out = out + placed(sums[:HIGH] + sums[HIGH : 2 * HIGH], 1)
-        out = out + placed(sums[2 * HIGH : 3 * HIGH] + sums[3 * HIGH :], 2)
-        out = out + placed(edge_sums[:HIGH] + edge_sums[HIGH:], 2)
+        out = out + folded(sums, 0, 1) + folded(sums, 2, 2)
+        out = out + padded(edge_sums[:HIGH] + edge_sums[HIGH:])
     mine[...] = out
 
     def share(step, carry):
@@ -325,7 +397,7 @@
         def _():
             pl.semaphore_wait(known.at[s], 1)
 
-    lax.fori_loop(1, count, share, 0)
+    lax.fori_loop(0, count - 1, share, 0)
     gathered[me] = mine[...]
     arrive(2, hx_z, hy_z)
     for s in (0, 1):
@@ -339,15 +411,14 @@
         dst_ref=others,
         send_sem=share_sem.at[0],
         recv_sem=share_sem.at[1],
-        device_id=peer(1),
+        device_id=peer(0),
         device_id_type=MESH,
     )
     shared.wait_recv()
     summed = jnp.sum(gathered[...], axis=0)
     first_lanes = lax.broadcasted_iota(jnp.int32, (HIGH, SKETCH), 1) < LOW
-    c0, c1 = coefficients(
-        *(jnp.where(first_lanes, pltpu.roll(summed, SKETCH - k * LOW, 1) if k else summed, 0.0) for k in range(3))
-    )
+    s0, s1, s2 = (jnp.where(first_lanes, pltpu.roll(summed, SKETCH - k * LOW, 1), 0.0) for k in (3, 1, 2))
+    c0, c1 = coefficients(s0, s1, s2 + jnp.where(first_lanes, summed, 0.0))
     for x in range(nx):
         answer[x] = c0 * r[x] + c1 * z1[x]
         rest[x] = r[x] - c0 * z1[x] - c1 * z2[x]
@@ -370,7 +441,7 @@
     count = ngx * ngy
     vm = lambda shape, dtype=f32: pltpu.VMEM(shape, dtype)
     block = (nx, ny, nz)
-    assert 2 * nx <= ny
+    assert 2 * nx <= ny and nx % 2 == 0
     answer, rest = pl.pallas_call(
         functools.partial(kernel, ngx, ngy, nx, ny, nz),
         out_shape=(vm(block), vm(block)),
@@ -381,14 +452,15 @@
             vm(block), vm(block), vm(block, jnp.int32), vm(block, jnp.int32), vm(block),
             vm(block), vm(block),
             vm((nx + 1, ny, nz)), vm(block), vm(block), vm(block), vm(block), vm((2, nx, nz)),
-            vm((nx, ny, LOW, nz), bf16), vm((3, ny, LOW, nz), bf16), vm((4, nx, ny, nz)), vm((2, 3, ny, nz)), vm((3, ny, nz), jnp.int32),
+            vm((nx, ny, WIDE, nz), bf16), vm((nx, ny, 2 * HIGH, nz), bf16), vm((3, ny, LOW, nz), bf16), vm((nx, nz // SKETCH, 4 * ny, SKETCH)), vm((2, 3, ny, nz)), vm((3, ny, nz), jnp.int32),
             vm((2, 2, ny, nz)), vm((2, 2, ny, nz)), vm((2, ny, nz)), vm((2, 2 * nx, nz)), vm((2, 2 * nx, nz)), vm((2, nx, nz)),
             vm((2, 2, ny, nz)), vm((2, 2, ny, nz)), vm((2, 2 * nx, nz)), vm((2, 2 * nx, nz)), vm((2, nx, nz)),
             vm((2, 5, ny, nz)), vm((2, 5, nx, nz)),
             vm((HIGH, SKETCH)), vm((count, HIGH, SKETCH)),
+            pltpu.SemaphoreType.DMA((3,)),
+            pltpu.SemaphoreType.DMA((2,)),
             pltpu.SemaphoreType.DMA((5,)),
             pltpu.SemaphoreType.DMA((2,)),
-            pltpu.SemaphoreType.DMA((2, 3)),
             pltpu.SemaphoreType.DMA((2,)),
             pltpu.SemaphoreType.REGULAR((2,)),
         ],

time: 15.2 us -> 14.8 us (0.974)
  Pallas kernels: 14.4 us -> 14 us
    pallas_call x1, Pallas kernels: 13.7 us -> 13.3 us  [body(): pl.pallas_call(functools.partial(kernel, ngx, ngy, nx, ny, nz), out_shape...]
where the time goes in v4:
time: 14.8 us; the launch traced here: 14.7 us
  Pallas kernels  14 us (95%)
  between operations  0.64 us (4%)
    pallas_call x1, Pallas kernels, body(): pl.pallas_call(functools.partial(kernel, ngx, ngy, nx, ny, nz), out_shape...  13.3 us
    pallas_call x1, Pallas kernels, body(): pl.pallas_call(put_out, out_shape=(jax.ShapeDtypeStruct(block, f32), jax....  0.72 us

profile of v4, /device:TPU:0, one launch (start us, length us, event | category | flops | bytes accessed | tf_op | source)
XLA Modules:
  0.0 14.7 jit_solution(14063640905607079251)
XLA Ops:
  0.6 13.3 %sketched_gmres.1 = (f32[4,8,1024]{2,1,0:T(8,128)S(1)}, f32[4,8,1024]{2,1,0:T(8,128)S(1)}) custom-call(f32[4,8,1024]{2,1,0:T(8,128)} %f_hbm.1, f32[4,8,1024]{2,1,0:T(8,128)} %w_hbm.1, s32[4,8,1024]{2,1,0:T(8,128)} %m_hbm.1, s32[4,8,1024]{2,1,0:T(8,128)} %s_hbm.1, f32[4,8,1024]{2,1,0:T(8,128)} %d_hbm.1), custom_call_target="tpu_custom_call" | custom-call | tf_op jit(solution)/shard_map/sketched_gmres/pallas_call | solution.py:445
  13.9 0.7 %put_out.1 = (f32[4,8,1024]{2,1,0:T(8,128)}, f32[4,8,1024]{2,1,0:T(8,128)}) custom-call(f32[4,8,1024]{2,1,0:T(8,128)S(1)} %get-tuple-element.4.answer, f32[4,8,1024]{2,1,0:T(8,128)S(1)} %get-tuple-element.5.rest), custom_call_target="tpu_custom_call" | custom-call | tf_op jit(solution)/shard_map/put_out/pallas_call | solution.py:470

commit v5 on v4

--- a/solution.py
+++ b/solution.py
@@ -48,7 +48,7 @@
 def kernel(
     ngx, ngy, nx, ny, nz,
     f_hbm, w_hbm, m_hbm, s_hbm, d_hbm,
-    answer, rest,
+    kept,
     z1, z2, r, w, m, slot, d, cond, diag, lx, ly, lydown, lz, lzleft, lyb, onehot, highs, onehot_edge, parts, wedge, sedge,
     hx_first, hx_early, hx_z, hy_first, hy_early, hy_z,
     px_first, px_early, py_first, py_early, py_z,
@@ -84,7 +84,7 @@
 
     loads = [
         pltpu.make_async_copy(src, dst, load_sem.at[i])
-        for i, src, dst in ((0, w_hbm, w), (0, m_hbm, m), (1, f_hbm, r), (2, s_hbm, slot), (2, d_hbm, d))
+        for i, src, dst in ((0, w_hbm, w), (0, m_hbm, m), (0, f_hbm, r), (1, s_hbm, slot), (1, d_hbm, d))
     ]
     for load in loads:
         load.start()
@@ -154,16 +154,14 @@
         )
         pl.when(jnp.logical_or(jnp.logical_and(side == 0, has_x[0]), jnp.logical_and(side == 1, has_x[1])))(copy.wait_recv)
 
-    two_blocks = parts.at[pl.ds(0, nx // 2)]
-
-    def both_loaded(i):
-        pltpu.make_async_copy(two_blocks, two_blocks, load_sem.at[i]).wait()
-
-    both_loaded(0)
+    def loaded(i, blocks):
+        size = parts.at[pl.ds(0, blocks * nx // 4)]
+        pltpu.make_async_copy(size, size, load_sem.at[i]).wait()
+
+    loaded(0, 3)
     for x in range(nx):
         phase = m[x]
         cond[x] = jnp.where(phase == 0, 0.2, jnp.where(phase == 1, 1.0, 0.6)).astype(f32) * (0.5 + w[x])
-    loads[2].wait()
     for s in (0, 1):
         e = edge_x[s]
         px_first[s, 0] = cond[e]
@@ -172,24 +170,12 @@
             py_first[s, pl.ds(x, 1), :] = r[x, pl.ds(edge_y[s], 1), :]
             py_first[s, pl.ds(nx + x, 1), :] = cond[x, pl.ds(edge_y[s], 1), :]
 
-        @pl.when(jnp.logical_not(has_x[s]))
-        def _():
-            hx_first[s] = jnp.zeros((2, ny, nz), f32)
-            hx_early[s] = jnp.zeros((2, ny, nz), f32)
-            hx_z[s] = jnp.zeros((ny, nz), f32)
-
-        @pl.when(jnp.logical_not(has_y[s]))
-        def _():
-            hy_first[s] = jnp.zeros((2 * nx, nz), f32)
-            hy_early[s] = jnp.zeros((2 * nx, nz), f32)
-            hy_z[s] = jnp.zeros((nx, nz), f32)
-
     pl.semaphore_wait(barrier, ngx - 1 + n_y)
     begin(0, lambda s: px_first.at[s], hx_first, lambda s: py_first.at[s], hy_first)
     if ngy > 1:
         pl.when(gy == 0)(functools.partial(tell, 1))
         pl.when(gy == ngy - 1)(functools.partial(tell, 0))
-    both_loaded(2)
+    loaded(1, 2)
     for s in (0, 1):
         e = edge_x[s]
         px_early[s, 0] = slot[e].astype(f32)
@@ -198,6 +184,20 @@
             py_early[s, pl.ds(x, 1), :] = slot[x, pl.ds(edge_y[s], 1), :].astype(f32)
             py_early[s, pl.ds(nx + x, 1), :] = d[x, pl.ds(edge_y[s], 1), :]
     begin(1, lambda s: px_early.at[s], hx_early, lambda s: py_early.at[s], hy_early)
+
+    for s in (0, 1):
+
+        @pl.when(jnp.logical_not(has_x[s]))
+        def _():
+            hx_first[s] = jnp.zeros((2, ny, nz), f32)
+            hx_early[s] = jnp.zeros((2, ny, nz), f32)
+            hx_z[s] = jnp.zeros((ny, nz), f32)
+
+        @pl.when(jnp.logical_not(has_y[s]))
+        def _():
+            hy_first[s] = jnp.zeros((2 * nx, nz), f32)
+            hy_early[s] = jnp.zeros((2 * nx, nz), f32)
+            hy_z[s] = jnp.zeros((nx, nz), f32)
 
     lane = lax.broadcasted_iota(jnp.int32, (ny, nz), 1)
     row = lax.broadcasted_iota(jnp.int32, (ny, nz), 0)
@@ -315,7 +315,13 @@
         pl.when(middle)(functools.partial(pass_on, 1))
         pl.when(middle)(functools.partial(pass_on, 0))
 
+    def place_edge(t, rows):
+        for y in range(rows):
+            onehot_edge[t, y] = low_rows(sedge.at[t], y)
+
     arrive_beside(near)
+    sedge[0] = hx_early[near, 0].astype(jnp.int32)
+    place_edge(0, ny)
     arrive(0, hx_first, hy_first)
     for s in (0, 1):
         e = edge_x[s]
@@ -350,18 +356,15 @@
 
     def sketch_edge(t, rows):
         for y in range(rows):
-            onehot_edge[t, y] = low_rows(sedge.at[t], y)
-        for y in range(rows):
             edge_chains[y % 2] = add_row(
                 edge_chains[y % 2], sedge.at[t], (wedge.at[0, t], wedge.at[1, t]), onehot_edge[t, y], y
             )
 
-    def face_edge(t, side):
+    def weigh_face(t, side):
         split(wedge.at[0, t], wedge.at[1, t], -lx[nx * side] * z1[(nx - 1) * side] * hx_early[side, 1])
-        sedge[t] = hx_early[side, 0].astype(jnp.int32)
-        sketch_edge(t, ny)
-
-    face_edge(0, near)
+
+    weigh_face(0, near)
+    sketch_edge(0, ny)
     settle(1, has_y, arrival(1, 1, 0), hy_early, "wait_recv")
     for s in (0, 1):
         for x in range(nx):
@@ -371,9 +374,13 @@
             wedge[0, 1, at, :] = upper
             wedge[1, 1, at, :] = edge - upper
             sedge[1, at, :] = hy_early[s, pl.ds(x, 1), :].astype(jnp.int32)
+    place_edge(1, 2 * nx)
     sketch_edge(1, 2 * nx)
     arrive_beside(far)
-    face_edge(2, far)
+    sedge[2] = hx_early[far, 0].astype(jnp.int32)
+    place_edge(2, ny)
+    weigh_face(2, far)
+    sketch_edge(2, ny)
     out = mine[...]
     for sums, edge_sums in zip(chains, edge_chains):
         out = out + folded(sums, 0, 1) + folded(sums, 2, 2)
@@ -420,20 +427,17 @@
     s0, s1, s2 = (jnp.where(first_lanes, pltpu.roll(summed, SKETCH - k * LOW, 1), 0.0) for k in (3, 1, 2))
     c0, c1 = coefficients(s0, s1, s2 + jnp.where(first_lanes, summed, 0.0))
     for x in range(nx):
-        answer[x] = c0 * r[x] + c1 * z1[x]
-        rest[x] = r[x] - c0 * z1[x] - c1 * z2[x]
+        kept[0, x] = c0 * r[x] + c1 * z1[x]
+        kept[1, x] = r[x] - c0 * z1[x] - c1 * z2[x]
     shared.wait_send()
     settle(0, has_x, sent.at[0], bulk_x, "wait_send")
     settle(1, has_y, sent.at[1], bulk_y, "wait_send")
 
 
-def put_out(answer, rest, answer_out, rest_out, sem):
-    one = pltpu.make_async_copy(answer, answer_out, sem.at[0])
-    two = pltpu.make_async_copy(rest, rest_out, sem.at[1])
-    one.start()
-    two.start()
-    one.wait()
-    two.wait()
+def put_out(kept, answer_out, rest_out, sem):
+    pltpu.make_async_copy(kept.at[0], answer_out, sem.at[0]).start()
+    pltpu.make_async_copy(kept.at[1], rest_out, sem.at[0]).start()
+    pltpu.make_async_copy(kept, kept, sem.at[0]).wait()
 
 
 def body(ngx, ngy, f, w, m, s, d):
@@ -441,12 +445,12 @@
     count = ngx * ngy
     vm = lambda shape, dtype=f32: pltpu.VMEM(shape, dtype)
     block = (nx, ny, nz)
-    assert 2 * nx <= ny and nx % 2 == 0
-    answer, rest = pl.pallas_call(
+    assert 2 * nx <= ny and nx % 4 == 0
+    kept = pl.pallas_call(
         functools.partial(kernel, ngx, ngy, nx, ny, nz),
-        out_shape=(vm(block), vm(block)),
+        out_shape=vm((2,) + block),
         in_specs=[pl.BlockSpec(memory_space=pl.ANY)] * 5,
-        out_specs=[pl.BlockSpec(memory_space=pltpu.VMEM)] * 2,
+        out_specs=pl.BlockSpec(memory_space=pltpu.VMEM),
         scratch_shapes=[
             vm(block), vm(block),
             vm(block), vm(block), vm(block, jnp.int32), vm(block, jnp.int32), vm(block),
@@ -457,7 +461,7 @@
             vm((2, 2, ny, nz)), vm((2, 2, ny, nz)), vm((2, 2 * nx, nz)), vm((2, 2 * nx, nz)), vm((2, nx, nz)),
             vm((2, 5, ny, nz)), vm((2, 5, nx, nz)),
             vm((HIGH, SKETCH)), vm((count, HIGH, SKETCH)),
-            pltpu.SemaphoreType.DMA((3,)),
+            pltpu.SemaphoreType.DMA((2,)),
             pltpu.SemaphoreType.DMA((2,)),
             pltpu.SemaphoreType.DMA((5,)),
             pltpu.SemaphoreType.DMA((2,)),
@@ -470,11 +474,11 @@
     return pl.pallas_call(
         put_out,
         out_shape=(jax.ShapeDtypeStruct(block, f32), jax.ShapeDtypeStruct(block, f32)),
-        in_specs=[pl.BlockSpec(memory_space=pltpu.VMEM)] * 2,
+        in_specs=[pl.BlockSpec(memory_space=pltpu.VMEM)],
         out_specs=[pl.BlockSpec(memory_space=pl.ANY)] * 2,
-        scratch_shapes=[pltpu.SemaphoreType.DMA((2,))],
+        scratch_shapes=[pltpu.SemaphoreType.DMA((1,))],
         name="put_out",
-    )(pltpu.with_memory_space_constraint(answer, pltpu.VMEM), pltpu.with_memory_space_constraint(rest, pltpu.VMEM))
+    )(pltpu.with_memory_space_constraint(kept, pltpu.VMEM))
 
 
 def solution(mesh):

time: 14.8 us -> 14.8 us (level)
  no operation moved by 1% of the time
where the time goes in v5:
time: 14.8 us; the launch traced here: 14.6 us
  Pallas kernels  14 us (95%)
  between operations  0.64 us (4%)
    pallas_call x1, Pallas kernels, body(): pl.pallas_call(functools.partial(kernel, ngx, ngy, nx, ny, nz), out_shape...  13.3 us
    pallas_call x1, Pallas kernels, body(): pl.pallas_call(put_out, out_shape=(jax.ShapeDtypeStruct(block, f32), jax....  0.71 us

profile of v5, /device:TPU:0, one launch (start us, length us, event | category | flops | bytes accessed | tf_op | source)
XLA Modules:
  0.0 14.6 jit_solution(2442014108122354102)
XLA Ops:
  0.6 13.3 %sketched_gmres.1.kept = f32[2,4,8,1024]{3,2,1,0:T(8,128)S(1)} custom-call(f32[4,8,1024]{2,1,0:T(8,128)} %f_hbm.1, f32[4,8,1024]{2,1,0:T(8,128)} %w_hbm.1, s32[4,8,1024]{2,1,0:T(8,128)} %m_hbm.1, s32[4,8,1024]{2,1,0:T(8,128)} %s_hbm.1, f32[4,8,1024]{2,1,0:T(8,128)} %d_hbm.1), custom_call_target="tpu_custom_call" | custom-call | tf_op jit(solution)/shard_map/sketched_gmres/pallas_call | solution.py:449
  13.9 0.7 %put_out.1 = (f32[4,8,1024]{2,1,0:T(8,128)}, f32[4,8,1024]{2,1,0:T(8,128)}) custom-call(f32[2,4,8,1024]{3,2,1,0:T(8,128)S(1)} %sketched_gmres.1.kept), custom_call_target="tpu_custom_call" | custom-call | tf_op jit(solution)/shard_map/put_out/pallas_call | solution.py:474

commit v6 on v4

--- a/solution.py
+++ b/solution.py
@@ -172,18 +172,6 @@
             py_first[s, pl.ds(x, 1), :] = r[x, pl.ds(edge_y[s], 1), :]
             py_first[s, pl.ds(nx + x, 1), :] = cond[x, pl.ds(edge_y[s], 1), :]
 
-        @pl.when(jnp.logical_not(has_x[s]))
-        def _():
-            hx_first[s] = jnp.zeros((2, ny, nz), f32)
-            hx_early[s] = jnp.zeros((2, ny, nz), f32)
-            hx_z[s] = jnp.zeros((ny, nz), f32)
-
-        @pl.when(jnp.logical_not(has_y[s]))
-        def _():
-            hy_first[s] = jnp.zeros((2 * nx, nz), f32)
-            hy_early[s] = jnp.zeros((2 * nx, nz), f32)
-            hy_z[s] = jnp.zeros((nx, nz), f32)
-
     pl.semaphore_wait(barrier, ngx - 1 + n_y)
     begin(0, lambda s: px_first.at[s], hx_first, lambda s: py_first.at[s], hy_first)
     if ngy > 1:
@@ -198,6 +186,20 @@
             py_early[s, pl.ds(x, 1), :] = slot[x, pl.ds(edge_y[s], 1), :].astype(f32)
             py_early[s, pl.ds(nx + x, 1), :] = d[x, pl.ds(edge_y[s], 1), :]
     begin(1, lambda s: px_early.at[s], hx_early, lambda s: py_early.at[s], hy_early)
+
+    for s in (0, 1):
+
+        @pl.when(jnp.logical_not(has_x[s]))
+        def _():
+            hx_first[s] = jnp.zeros((2, ny, nz), f32)
+            hx_early[s] = jnp.zeros((2, ny, nz), f32)
+            hx_z[s] = jnp.zeros((ny, nz), f32)
+
+        @pl.when(jnp.logical_not(has_y[s]))
+        def _():
+            hy_first[s] = jnp.zeros((2 * nx, nz), f32)
+            hy_early[s] = jnp.zeros((2 * nx, nz), f32)
+            hy_z[s] = jnp.zeros((nx, nz), f32)
 
     lane = lax.broadcasted_iota(jnp.int32, (ny, nz), 1)
     row = lax.broadcasted_iota(jnp.int32, (ny, nz), 0)
@@ -315,7 +317,13 @@
         pl.when(middle)(functools.partial(pass_on, 1))
         pl.when(middle)(functools.partial(pass_on, 0))
 
+    def place_edge(t, rows):
+        for y in range(rows):
+            onehot_edge[t, y] = low_rows(sedge.at[t], y)
+
     arrive_beside(near)
+    sedge[0] = hx_early[near, 0].astype(jnp.int32)
+    place_edge(0, ny)
     arrive(0, hx_first, hy_first)
     for s in (0, 1):
         e = edge_x[s]
@@ -333,6 +341,11 @@
             py_z[s, here, :] = after
     begin(2, lambda s: z1.at[edge_x[s]], hx_z, lambda s: py_z.at[s], hy_z)
     chains = [jnp.zeros((2 * HIGH, WIDE), f32) for _ in range(2)]
+
+    def sketch_plane(x):
+        for y in range(ny):
+            chains[y % 2] = chains[y % 2] + matmul(masked(x, y), onehot[x, y])
+
     for x in range(nx):
         out = apply(z1, x)
         for s in (0, 1):
@@ -344,25 +357,23 @@
             z2[at] = z2[at] + lyb[s, pl.ds(x, 1), :] * py_z[s, pl.ds(x, 1), :]
         split_into(x, 0, d[x] * z1[x])
         split_into(x, 2, d[x] * z2[x])
-        for y in range(ny):
-            chains[y % 2] = chains[y % 2] + matmul(masked(x, y), onehot[x, y])
+        if x < 2:
+            sketch_plane(x)
     edge_chains = [jnp.zeros((2 * HIGH, LOW), f32) for _ in range(2)]
 
     def sketch_edge(t, rows):
-        for y in range(rows):
-            onehot_edge[t, y] = low_rows(sedge.at[t], y)
         for y in range(rows):
             edge_chains[y % 2] = add_row(
                 edge_chains[y % 2], sedge.at[t], (wedge.at[0, t], wedge.at[1, t]), onehot_edge[t, y], y
             )
 
-    def face_edge(t, side):
+    def weigh_face(t, side):
         split(wedge.at[0, t], wedge.at[1, t], -lx[nx * side] * z1[(nx - 1) * side] * hx_early[side, 1])
-        sedge[t] = hx_early[side, 0].astype(jnp.int32)
-        sketch_edge(t, ny)
-
-    face_edge(0, near)
+
+    weigh_face(0, near)
+    sketch_edge(0, ny)
     settle(1, has_y, arrival(1, 1, 0), hy_early, "wait_recv")
+    arrive_beside(far)
     for s in (0, 1):
         for x in range(nx):
             at = pl.ds(s * nx + x, 1)
@@ -371,9 +382,14 @@
             wedge[0, 1, at, :] = upper
             wedge[1, 1, at, :] = edge - upper
             sedge[1, at, :] = hy_early[s, pl.ds(x, 1), :].astype(jnp.int32)
+    place_edge(1, 2 * nx)
+    for x in range(2, nx):
+        sketch_plane(x)
     sketch_edge(1, 2 * nx)
-    arrive_beside(far)
-    face_edge(2, far)
+    sedge[2] = hx_early[far, 0].astype(jnp.int32)
+    place_edge(2, ny)
+    weigh_face(2, far)
+    sketch_edge(2, ny)
     out = mine[...]
     for sums, edge_sums in zip(chains, edge_chains):
         out = out + folded(sums, 0, 1) + folded(sums, 2, 2)

time: 14.8 us -> 14.7 us (level)
  no operation moved by 1% of the time
where the time goes in v6:
time: 14.7 us; the launch traced here: 14.6 us
  Pallas kernels  14 us (95%)
  between operations  0.64 us (4%)
    pallas_call x1, Pallas kernels, body(): pl.pallas_call(functools.partial(kernel, ngx, ngy, nx, ny, nz), out_shape...  13.2 us
    pallas_call x1, Pallas kernels, body(): pl.pallas_call(put_out, out_shape=(jax.ShapeDtypeStruct(block, f32), jax....  0.72 us

profile of v6, /device:TPU:0, one launch (start us, length us, event | category | flops | bytes accessed | tf_op | source)
XLA Modules:
  0.0 14.6 jit_solution(3048589913580908619)
XLA Ops:
  0.6 13.2 %sketched_gmres.1 = (f32[4,8,1024]{2,1,0:T(8,128)S(1)}, f32[4,8,1024]{2,1,0:T(8,128)S(1)}) custom-call(f32[4,8,1024]{2,1,0:T(8,128)} %f_hbm.1, f32[4,8,1024]{2,1,0:T(8,128)} %w_hbm.1, s32[4,8,1024]{2,1,0:T(8,128)} %m_hbm.1, s32[4,8,1024]{2,1,0:T(8,128)} %s_hbm.1, f32[4,8,1024]{2,1,0:T(8,128)} %d_hbm.1), custom_call_target="tpu_custom_call" | custom-call | tf_op jit(solution)/shard_map/sketched_gmres/pallas_call | solution.py:461
  13.9 0.7 %put_out.1 = (f32[4,8,1024]{2,1,0:T(8,128)}, f32[4,8,1024]{2,1,0:T(8,128)}) custom-call(f32[4,8,1024]{2,1,0:T(8,128)S(1)} %get-tuple-element.4.answer, f32[4,8,1024]{2,1,0:T(8,128)S(1)} %get-tuple-element.5.rest), custom_call_target="tpu_custom_call" | custom-call | tf_op jit(solution)/shard_map/put_out/pallas_call | solution.py:486
